TPU v7x, 32 devices: a whole 2x2x4 slice. The times are simulated.
32 devices in a mesh: grp: 2 (over x), dev: 16 (over z, y, core).
Axes of the slice: x: 2, y: 2, z: 4, core: 2. Of those that a mesh axis runs over, the one named last changes fastest.
Arguments:
- coords: float32 [16384, 64], P(('grp', 'dev')), may hold values from -6 to 6
- right_side: float32 [16384, 256], P(('grp', 'dev')), may hold values from -6 to 6
- leaf_perm: int32 [32, 512], P(('grp', 'dev')), may hold values from 0 to 511, each once within a row
- near_list: int32 [32, 4], P(('grp', 'dev')), may hold values from -1 to 31, as said below
- far_leaves: int32 [32, 4], P(('grp', 'dev')), may hold values from 0 to 31, as said below
- couplings: bfloat16 [32, 4, 128, 128], P(('grp', 'dev')), may hold values from -0.5 to 0.5
- transfer: bfloat16 [32, 128, 128], P(('grp', 'dev')), may hold values from -0.5 to 0.5
- leaf_basis: bfloat16 [16384, 128], P(('grp', 'dev')), may hold values from -0.25 to 0.25
- cluster_of: int32 [32], P(('grp', 'dev')), may hold values from 0 to 7, as said below
- far_clusters: int32 [8, 4], P('grp'), may hold values from 0 to 7, as said below
- cluster_couplings: bfloat16 [8, 4, 128, 128], P('grp'), may hold values from -0.25 to 0.25
- ridge_weight: float32 [], replicated, may hold values from 0.5 to 2
Outputs:
- solution: float32 [16384, 256], P(('grp', 'dev'))
- residual: float32 [16384, 256], P(('grp', 'dev'))
Inputs may be any that keep to these rules, and one draw needn't show every extreme that they name: `near_list`: each row lists leaves of the row's group whose position within the group differs from the row's leaf by 1 to 2, each at most once, in any slot order; -1 marks an empty slot. The number of listed leaves varies from leaf to leaf. `far_leaves`: each row names 4 different leaves of the row's group whose position within the group differs from the row's leaf by more than 2 and at most 8. `cluster_of`: leaves of group g belong to clusters g * 4 to g * 4 + 3, and every cluster holds exactly 4 leaves. `far_clusters`: each row names 4 different clusters, none of them in the row's own group.
All inputs are finite; a program needn't handle non-finite values.
Results may differ from a plain program's by a relative error of at most 0.0033.
Values may be sent and summed in bfloat16 or wider, within the bound.
A program may use at most 64 MiB of HBM per device.

v0:
```python
import jax
import jax.numpy as jnp
from jax import lax
from jax.sharding import PartitionSpec as P

REACH = 2
FARREACH = 8
ITERS = 2


kernel_scale = 1.0 / 32.0
spectrum_gap = 0.5
spectrum_top = 8.0


def from_behind(shard, axis, by):
    devices = lax.axis_size(axis)
    pairs = [(i, i + by) for i in range(devices) if 0 <= i + by < devices]
    return lax.ppermute(shard, axis, pairs)


def kernel_block(left_points, right_points):
    inner_products = jnp.dot(
        left_points,
        right_points.T,
        precision=lax.Precision.HIGHEST,
        preferred_element_type=jnp.float32,
    )
    distance = (
        jnp.sum(left_points * left_points, axis=1)[:, None]
        + jnp.sum(right_points * right_points, axis=1)[None, :]
        - 2.0 * inner_products
    )
    return jnp.exp(-kernel_scale * distance).astype(jnp.bfloat16)


def body(
    coords,
    right_side,
    leaf_perm,
    near_list,
    far_leaves,
    couplings,
    transfer,
    leaf_basis,
    cluster_of,
    far_clusters,
    cluster_couplings,
    ridge_weight,
):
    dev_count = lax.axis_size("dev")
    group_index = lax.axis_index("grp")
    leaf_id = group_index * dev_count + lax.axis_index("dev")
    clusters_here = far_clusters.shape[0]
    local_cluster = cluster_of[0] - group_index * clusters_here
    ordering = leaf_perm[0]
    near_offsets = [offset for offset in range(-REACH, REACH + 1) if offset != 0]
    far_offsets = [offset for offset in range(-FARREACH, FARREACH + 1) if abs(offset) > REACH]
    neighbours = [from_behind(coords, "dev", -offset) for offset in near_offsets]
    near_flags = [
        jnp.any((near_list[0] == leaf_id + offset) & (near_list[0] >= 0)).astype(jnp.float32)
        for offset in near_offsets
    ]
    far_hits = jnp.stack(
        [far_leaves[0] == leaf_id + offset for offset in far_offsets], axis=1
    ).astype(jnp.bfloat16)
    own_block = kernel_block(coords, coords)
    near_blocks = [kernel_block(coords, neighbour_points) for neighbour_points in neighbours]
    cluster_slots = (jnp.arange(clusters_here) == local_cluster).astype(jnp.float32)

    def operate(direction):
        values = direction.astype(jnp.bfloat16)
        near_sum = jnp.dot(own_block, values, preferred_element_type=jnp.float32)
        for position in range(len(near_offsets)):
            remote = from_behind(values, "dev", -near_offsets[position])
            block_here = near_blocks[position]
            near_term = near_flags[position] * jnp.dot(
                block_here, remote, preferred_element_type=jnp.float32
            )
            near_sum = near_sum + near_term
        skeleton = lax.dot_general(
            leaf_basis,
            values[ordering],
            (((0,), (0,)), ((), ())),
            preferred_element_type=jnp.float32,
        ).astype(jnp.bfloat16)
        remote_skeletons = jnp.stack(
            [from_behind(skeleton, "dev", -offset) for offset in far_offsets]
        )
        chosen = jnp.einsum(
            "kj,jbo->kbo", far_hits, remote_skeletons, preferred_element_type=jnp.float32
        ).astype(jnp.bfloat16)
        level_one = jnp.einsum(
            "kab,kbo->ao", couplings[0], chosen, preferred_element_type=jnp.float32
        )
        uplift = lax.dot_general(
            transfer[0], skeleton, (((0,), (0,)), ((), ())), preferred_element_type=jnp.float32
        )
        contrib = cluster_slots[:, None, None] * uplift[None]
        column_sums = lax.psum_scatter(contrib, "dev", scatter_dimension=2, tiled=True).astype(
            jnp.bfloat16
        )
        every_column = lax.all_gather(column_sums, "grp", axis=0, tiled=True)
        picked = every_column[far_clusters]
        partial_coupled = jnp.einsum(
            "ckab,ckbo->cao", cluster_couplings, picked, preferred_element_type=jnp.float32
        ).astype(jnp.bfloat16)
        whole_columns = lax.all_gather(partial_coupled, "dev", axis=2, tiled=True)
        coupled = whole_columns[local_cluster]
        downward = jnp.dot(transfer[0], coupled, preferred_element_type=jnp.float32)
        tree_rows = jnp.dot(
            leaf_basis,
            (level_one + downward).astype(jnp.bfloat16),
            preferred_element_type=jnp.float32,
        )
        far_part = jnp.zeros_like(tree_rows).at[ordering].set(tree_rows)
        return ridge_weight * direction + (near_sum + far_part)

    bottom_edge = ridge_weight + spectrum_gap
    top_edge = ridge_weight + spectrum_top
    centre = (top_edge + bottom_edge) / 2.0
    spread = (top_edge - bottom_edge) / 2.0
    sigma_ratio = centre / spread
    contraction = 1.0 / sigma_ratio
    direction = right_side / centre
    solution = direction
    residual = right_side
    for rounds in range(ITERS):
        residual = residual - operate(direction)
        rho_next = 1.0 / (2.0 * sigma_ratio - contraction)
        direction = rho_next * contraction * direction + 2.0 * rho_next / spread * residual
        solution = solution + direction
        contraction = rho_next
    return (solution, residual)


def solution(mesh):
    placed = (
        P(("grp", "dev"), None),
        P(("grp", "dev"), None),
        P(("grp", "dev"), None),
        P(("grp", "dev"), None),
        P(("grp", "dev"), None),
        P(("grp", "dev"), None, None, None),
        P(("grp", "dev"), None, None),
        P(("grp", "dev"), None),
        P(("grp", "dev")),
        P("grp", None),
        P("grp", None, None, None),
        P(),
    )
    return jax.shard_map(
        body,
        mesh=mesh,
        in_specs=placed,
        out_specs=(P(("grp", "dev"), None), P(("grp", "dev"), None)),
        check_vma=False,
    )
```

profile of v0, /device:TPU:0, one launch (start us, length us, event | category | flops | bytes accessed | tf_op | source)
XLA Modules:
  0.0 243.9 jit_solution(6696561927409434020)
XLA Ops:
  8.6 1.1 fusion.53
  9.7 2.0 gather_fusion
  12.0 6.0 %collective-permute-start.8 = (bf16[128,256]{0,1:T(8,128)(2,1)S(1)}, bf16[128,256]{0,1:T(8,128)(2,1)S(1)}, u32[]{:S(2)}, u32[]{:S(2)}) collective-permute-start(bf16[128,256]{0,1:T(8,128)(2,1)S(1)} %bitcast.186), channel_id=1, source_target_pairs={{0,8},{1,9},{2,10},{3,11},{4,12},{5,13},{6,14},{7,15},{16,24},{17,... | collective-permute-start | bytes 196616 | tf_op jit(solution)/shard_map/ppermute | solution.py:19
  18.0 3.6 %collective-permute-start.9 = (bf16[128,256]{0,1:T(8,128)(2,1)S(1)}, bf16[128,256]{0,1:T(8,128)(2,1)S(1)}, u32[]{:S(2)}, u32[]{:S(2)}) collective-permute-start(bf16[128,256]{0,1:T(8,128)(2,1)S(1)} %bitcast.187), channel_id=1, source_target_pairs={{0,7},{1,8},{2,9},{3,10},{4,11},{5,12},{6,13},{7,14},{8,15},{16,23... | collective-permute-start | bytes 196616 | tf_op jit(solution)/shard_map/ppermute | solution.py:19
  21.6 2.1 collective-permute-start.10
  23.7 1.3 collective-permute-start.11
  25.0 1.6 collective-permute-start.12
  34.3 2.2 fusion.3
  38.8 2.9 %collective-permute-start.13 = (bf16[128,256]{0,1:T(8,128)(2,1)S(1)}, bf16[128,256]{0,1:T(8,128)(2,1)S(1)}, u32[]{:S(2)}, u32[]{:S(2)}) collective-permute-start(bf16[128,256]{0,1:T(8,128)(2,1)S(1)} %bitcast.191), channel_id=1, source_target_pairs={{0,3},{1,4},{2,5},{3,6},{4,7},{5,8},{6,9},{7,10},{8,11},{9,12},{10... | collective-permute-start | bytes 196616 | tf_op jit(solution)/shard_map/ppermute | solution.py:19
  42.4 1.3 collective-permute-start.14
  44.3 1.3 collective-permute-start.15
  46.2 1.3 collective-permute-start.16
  48.1 1.3 collective-permute-start.17
  50.1 1.3 collective-permute-start.18
  52.0 1.3 collective-permute-start.19
  53.9 2.8 %collective-permute-start.1 = (bf16[512,256]{1,0:T(8,128)(2,1)S(1)}, bf16[512,256]{1,0:T(8,128)(2,1)}, u32[]{:S(2)}, u32[]{:S(2)}) collective-permute-start(bf16[512,256]{1,0:T(8,128)(2,1)S(1)} %fusion.53), channel_id=1, source_target_pairs={{0,2},{1,3},{2,4},{3,5},{4,6},{5,7},{6,8},{7,9},{8,10},{9,11},{10,... | collective-permute-start | bytes 786440 | tf_op jit(solution)/shard_map/ppermute | solution.py:19
  57.4 5.4 %collective-permute-start = (f32[512,64]{0,1:T(8,128)}, f32[512,64]{0,1:T(8,128)S(1)}, u32[]{:S(2)}, u32[]{:S(2)}) collective-permute-start(f32[512,64]{0,1:T(8,128)} %param.12), channel_id=1, source_target_pairs={{0,2},{1,3},{2,4},{3,5},{4,6},{5,7},{6,8},{7,9},{8,10},{9,11},{10,... | collective-permute-start | bytes 393224 | tf_op jit(solution)/shard_map/ppermute | solution.py:19
  63.4 2.8 %collective-permute-start.3 = (bf16[512,256]{1,0:T(8,128)(2,1)S(1)}, bf16[512,256]{1,0:T(8,128)(2,1)}, u32[]{:S(2)}, u32[]{:S(2)}) collective-permute-start(bf16[512,256]{1,0:T(8,128)(2,1)S(1)} %fusion.53), channel_id=1, source_target_pairs={{0,1},{1,2},{2,3},{3,4},{4,5},{5,6},{6,7},{7,8},{8,9},{9,10},{10,1... | collective-permute-start | bytes 786440 | tf_op jit(solution)/shard_map/ppermute | solution.py:19
  66.8 4.2 %collective-permute-start.2 = (f32[512,64]{0,1:T(8,128)}, f32[512,64]{0,1:T(8,128)}, u32[]{:S(2)}, u32[]{:S(2)}) collective-permute-start(f32[512,64]{0,1:T(8,128)} %param.12), channel_id=1, source_target_pairs={{0,1},{1,2},{2,3},{3,4},{4,5},{5,6},{6,7},{7,8},{8,9},{9,10},{10,1... | collective-permute-start | bytes 393224 | tf_op jit(solution)/shard_map/ppermute | solution.py:19
  71.6 1.3 collective-permute-start.7
  73.5 2.0 copy.32
  76.7 1.3 collective-permute-start.6
  78.1 2.1 exponential_convert_fusion.3
  80.2 1.3 collective-permute-start.5
  82.4 2.1 exponential_convert_fusion.2
  84.6 1.2 collective-permute-done.6
  85.8 1.3 collective-permute-start.4
  87.1 2.1 exponential_convert_fusion
  89.3 2.9 %exponential_convert_fusion.1 = bf16[512,512]{1,0:T(8,128)(2,1)} fusion(f32[512]{0:T(512)S(1)} %multiply_reduce_fusion.1, f32[512,64]{0,1:T(8,128)} %param.12, f32[512,64]{0,1:T(8,128)S(1)} %collective-permute-done.4, f32[512]{0:T(512)S(1)} %copy-done.15), kind=kOutput, calls=%fused_computation.58 | convolution fusion | flops 202637312 | bytes 790528 | tf_op jit(solution)/shard_map/dot_general | solution.py:23
  92.2 1.2 fusion.17
  93.5 1.2 convolution_multiply_fusion.9
  94.7 2.0 fusion.16
  97.6 4.4 %all_gather.12 = bf16[8,128,16]{1,2,0:T(8,128)(2,1)S(1)} all-gather(bf16[4,128,16]{1,2,0:T(8,128)(2,1)S(1)} %convert_element_type.99), channel_id=1, replica_groups=mesh['grp'=2,'dev'=16] {'grp'}, dimensions={0}, use_global_device_ids=true | all-gather | bytes 49152 | tf_op jit(solution)/shard_map/all_gather | solution.py:103
  102.8 28.1 %all_gather.13 = bf16[4,128,256]{1,2,0:T(8,128)(2,1)S(1)} all-gather(bf16[4,128,16]{1,2,0:T(8,128)(2,1)S(1)} %fusion.23), channel_id=1, replica_groups=mesh['grp'=2,'dev'=16] {'dev'}, dimensions={2}, use_global_device_ids=true | all-gather | bytes 278528 | tf_op jit(solution)/shard_map/all_gather | solution.py:108
  132.2 2.9 %scatter_custom_fusion = f32[512,256]{1,0:T(8,128)S(1)} fusion(s32[512]{0:T(512)S(1)} %bitcast.211, f32[512,256]{1,0:T(8,128)} %copy.34, f32[]{:T(128)} %constant.33.clone.1), kind=kCustom, calls=%fused_computation.70 | custom fusion | bytes 524800 | tf_op jit(solution)/shard_map/scatter | solution.py:116
  135.2 2.4 %fusion.24 = (bf16[512,256]{1,0:T(8,128)(2,1)S(1)}, f32[512,256]{1,0:T(8,128)}) fusion(f32[]{:T(128)S(6)} %div.37, f32[]{:T(128)S(6)} %mul.171, f32[512,256]{1,0:T(8,128)S(1)} %copy-done.10, f32[]{:T(128)S(6)} %div.30, f32[512,256]{1,0:T(8,128)S(1)} %scatter_custom_fusion, f32[512,256]{1,0:T(8,128)S(1)} %convolution_multiply_fusion.9, ...), kind=kOutput, calls=%fused_computation.63 | convolution fusion | flops 135790592 | bytes 3670036 | tf_op jit(solution)/shard_map/dot_general | solution.py:77
  137.9 2.0 collective-permute-start.20
  139.9 2.9 %collective-permute-start.21 = (bf16[512,256]{1,0:T(8,128)(2,1)S(1)}, bf16[512,256]{1,0:T(8,128)(2,1)}, u32[]{:S(2)}, u32[]{:S(2)}) collective-permute-start(bf16[512,256]{1,0:T(8,128)(2,1)S(1)} %get-tuple-element.18), channel_id=1, source_target_pairs={{0,1},{1,2},{2,3},{3,4},{4,5},{5,6},{6,7},{7,8},{8,9},{9,10},{10,1... | collective-permute-start | bytes 786440 | tf_op jit(solution)/shard_map/ppermute | solution.py:19
  142.9 1.9 gather_fusion.2
  145.1 1.3 collective-permute-start.24
  146.4 1.3 collective-permute-start.25
  147.7 2.3 collective-permute-start.26
  151.1 1.8 collective-permute-start.27
  153.5 2.3 collective-permute-start.28
  156.5 3.0 %collective-permute-start.29 = (bf16[128,256]{0,1:T(8,128)(2,1)S(1)}, bf16[128,256]{0,1:T(8,128)(2,1)S(1)}, u32[]{:S(2)}, u32[]{:S(2)}) collective-permute-start(bf16[128,256]{0,1:T(8,128)(2,1)S(1)} %bitcast.203), channel_id=1, source_target_pairs={{0,3},{1,4},{2,5},{3,6},{4,7},{5,8},{6,9},{7,10},{8,11},{9,12},{10... | collective-permute-start | bytes 196616 | tf_op jit(solution)/shard_map/ppermute | solution.py:19
  160.1 1.3 collective-permute-start.30
  162.1 1.3 collective-permute-start.31
  164.0 1.3 collective-permute-start.32
  165.9 1.3 collective-permute-start.33
  168.8 1.3 collective-permute-start.34
  171.5 1.3 collective-permute-start.35
  173.5 2.0 collective-permute-done.33
  175.5 1.3 collective-permute-start.23
  177.4 1.3 collective-permute-start.22
  179.3 5.8 %collective-permute-done.35 = bf16[128,256]{0,1:T(8,128)(2,1)S(1)} collective-permute-done((bf16[128,256]{0,1:T(8,128)(2,1)S(1)}, bf16[128,256]{0,1:T(8,128)(2,1)S(1)}, u32[]{:S(2)}, u32[]{:S(2)}) %collective-permute-start.35) | collective-permute-done | bytes 65568 | tf_op jit(solution)/shard_map/ppermute | solution.py:19
  185.7 2.0 copy.35
  189.6 1.2 fusion.10
  190.9 1.3 convolution_multiply_fusion.5
  192.2 1.3 fusion.9
  193.5 11.7 %reduce-scatter.5.cloned.1.call-done = f32[4,128,16]{1,2,0:T(8,128)} async-done(((f32[4,128,256]{1,2,0:T(8,128)}), f32[4,128,16]{1,2,0:T(8,128)}) %reduce-scatter.5.cloned.1.call-update) | async-done | bytes 32784 | tf_op jit(solution)/shard_map/reduce_scatter | solution.py:100
  206.0 4.4 %all_gather.14 = bf16[8,128,16]{1,2,0:T(8,128)(2,1)S(1)} all-gather(bf16[4,128,16]{1,2,0:T(8,128)(2,1)S(1)} %convert_element_type.107), channel_id=1, replica_groups=mesh['grp'=2,'dev'=16] {'grp'}, dimensions={0}, use_global_device_ids=true | all-gather | bytes 49152 | tf_op jit(solution)/shard_map/all_gather | solution.py:103
  211.2 20.3 %all_gather.15 = bf16[4,128,256]{1,2,0:T(8,128)(2,1)S(1)} all-gather(bf16[4,128,16]{1,2,0:T(8,128)(2,1)S(1)} %fusion.22), channel_id=1, replica_groups=mesh['grp'=2,'dev'=16] {'dev'}, dimensions={2}, use_global_device_ids=true | all-gather | bytes 278528 | tf_op jit(solution)/shard_map/all_gather | solution.py:108
  232.0 2.4 scatter_custom_fusion.1
  234.4 2.7 %add_add_fusion = (f32[512,256]{1,0:T(8,128)}, f32[512,256]{1,0:T(8,128)}) fusion(f32[512,256]{1,0:T(8,128)} %get-tuple-element.19, f32[]{:T(128)S(6)} %div.39, f32[]{:T(128)S(6)} %mul.207, f32[]{:T(128)S(6)} %div.37, f32[]{:T(128)S(6)} %mul.171, f32[512,256]{1,0:T(8,128)S(1)} %copy-done.11, f32[]{:T(128)S(6)} %div.30, ...), kind=kOutput, calls=%fused_computation.61 | convolution fusion | flops 136314880 | bytes 4456476 | tf_op jit(solution)/shard_map/dot_general | solution.py:77
  (154 shorter events, 35.3 us)
Async XLA Ops:
  7.2 95.4 %copy-start = (bf16[4,4,128,128]{3,2,1,0:T(8,128)(2,1)S(1)}, bf16[4,4,128,128]{3,2,1,0:T(8,128)(2,1)}, u32[]{:S(2)}) copy-start(bf16[4,4,128,128]{3,2,1,0:T(8,128)(2,1)} %param.22) | copy-start | bytes 1572868
  7.2 89.6 %reduce-scatter.3.cloned.1.call-start = ((), (), s32[]{:S(2)}) async-start(), calls=%async_computation.2 | async-start | bytes 557056 | tf_op jit(solution)/shard_map/reduce_scatter | solution.py:100
  7.9 0.7 copy-start.16
  9.7 2.0 copy-start.1
  11.7 15.0 %copy-start.6 = (bf16[1,128,128]{2,1,0:T(8,128)(2,1)S(1)}, bf16[1,128,128]{2,1,0:T(8,128)(2,1)}, u32[]{:S(2)}) copy-start(bf16[1,128,128]{2,1,0:T(8,128)(2,1)} %param.18) | copy-start | bytes 98308
  12.0 26.9 %collective-permute-start.8 = (bf16[128,256]{0,1:T(8,128)(2,1)S(1)}, bf16[128,256]{0,1:T(8,128)(2,1)S(1)}, u32[]{:S(2)}, u32[]{:S(2)}) collective-permute-start(bf16[128,256]{0,1:T(8,128)(2,1)S(1)} %bitcast.186), channel_id=1, source_target_pairs={{0,8},{1,9},{2,10},{3,11},{4,12},{5,13},{6,14},{7,15},{16,24},{17,... | collective-permute-start | bytes 196616 | tf_op jit(solution)/shard_map/ppermute | solution.py:19
  18.0 24.4 %collective-permute-start.9 = (bf16[128,256]{0,1:T(8,128)(2,1)S(1)}, bf16[128,256]{0,1:T(8,128)(2,1)S(1)}, u32[]{:S(2)}, u32[]{:S(2)}) collective-permute-start(bf16[128,256]{0,1:T(8,128)(2,1)S(1)} %bitcast.187), channel_id=1, source_target_pairs={{0,7},{1,8},{2,9},{3,10},{4,11},{5,12},{6,13},{7,14},{8,15},{16,23... | collective-permute-start | bytes 196616 | tf_op jit(solution)/shard_map/ppermute | solution.py:19
  21.6 22.7 %collective-permute-start.10 = (bf16[128,256]{0,1:T(8,128)(2,1)S(1)}, bf16[128,256]{0,1:T(8,128)(2,1)S(1)}, u32[]{:S(2)}, u32[]{:S(2)}) collective-permute-start(bf16[128,256]{0,1:T(8,128)(2,1)S(1)} %bitcast.188), channel_id=1, source_target_pairs={{0,6},{1,7},{2,8},{3,9},{4,10},{5,11},{6,12},{7,13},{8,14},{9,15},... | collective-permute-start | bytes 196616 | tf_op jit(solution)/shard_map/ppermute | solution.py:19
  23.7 22.5 %collective-permute-start.11 = (bf16[128,256]{0,1:T(8,128)(2,1)S(1)}, bf16[128,256]{0,1:T(8,128)(2,1)S(1)}, u32[]{:S(2)}, u32[]{:S(2)}) collective-permute-start(bf16[128,256]{0,1:T(8,128)(2,1)S(1)} %bitcast.189), channel_id=1, source_target_pairs={{0,5},{1,6},{2,7},{3,8},{4,9},{5,10},{6,11},{7,12},{8,13},{9,14},{... | collective-permute-start | bytes 196616 | tf_op jit(solution)/shard_map/ppermute | solution.py:19
  25.0 23.1 %collective-permute-start.12 = (bf16[128,256]{0,1:T(8,128)(2,1)S(1)}, bf16[128,256]{0,1:T(8,128)(2,1)S(1)}, u32[]{:S(2)}, u32[]{:S(2)}) collective-permute-start(bf16[128,256]{0,1:T(8,128)(2,1)S(1)} %bitcast.190), channel_id=1, source_target_pairs={{0,4},{1,5},{2,6},{3,7},{4,8},{5,9},{6,10},{7,11},{8,12},{9,13},{1... | collective-permute-start | bytes 196616 | tf_op jit(solution)/shard_map/ppermute | solution.py:19
  27.5 0.9 copy-start.18
  28.4 176.8 %reduce-scatter.5.cloned.1.call-start = ((), (), s32[]{:S(2)}) async-start(), calls=%async_computation.3 | async-start | bytes 557056 | tf_op jit(solution)/shard_map/reduce_scatter | solution.py:100
  28.7 0.7 copy-start.20
  30.5 0.7 copy-start.17
  31.3 0.7 copy-start.21
  34.3 2.2 copy-start.14
  38.8 11.2 %collective-permute-start.13 = (bf16[128,256]{0,1:T(8,128)(2,1)S(1)}, bf16[128,256]{0,1:T(8,128)(2,1)S(1)}, u32[]{:S(2)}, u32[]{:S(2)}) collective-permute-start(bf16[128,256]{0,1:T(8,128)(2,1)S(1)} %bitcast.191), channel_id=1, source_target_pairs={{0,3},{1,4},{2,5},{3,6},{4,7},{5,8},{6,9},{7,10},{8,11},{9,12},{10... | collective-permute-start | bytes 196616 | tf_op jit(solution)/shard_map/ppermute | solution.py:19
  42.4 9.6 %collective-permute-start.14 = (bf16[128,256]{0,1:T(8,128)(2,1)S(1)}, bf16[128,256]{0,1:T(8,128)(2,1)S(1)}, u32[]{:S(2)}, u32[]{:S(2)}) collective-permute-start(bf16[128,256]{0,1:T(8,128)(2,1)S(1)} %bitcast.192), channel_id=1, source_target_pairs={{3,0},{4,1},{5,2},{6,3},{7,4},{8,5},{9,6},{10,7},{11,8},{12,9},{13... | collective-permute-start | bytes 196616 | tf_op jit(solution)/shard_map/ppermute | solution.py:19
  44.3 9.6 %collective-permute-start.15 = (bf16[128,256]{0,1:T(8,128)(2,1)S(1)}, bf16[128,256]{0,1:T(8,128)(2,1)S(1)}, u32[]{:S(2)}, u32[]{:S(2)}) collective-permute-start(bf16[128,256]{0,1:T(8,128)(2,1)S(1)} %bitcast.193), channel_id=1, source_target_pairs={{4,0},{5,1},{6,2},{7,3},{8,4},{9,5},{10,6},{11,7},{12,8},{13,9},{1... | collective-permute-start | bytes 196616 | tf_op jit(solution)/shard_map/ppermute | solution.py:19
  46.2 11.1 %collective-permute-start.16 = (bf16[128,256]{0,1:T(8,128)(2,1)S(1)}, bf16[128,256]{0,1:T(8,128)(2,1)S(1)}, u32[]{:S(2)}, u32[]{:S(2)}) collective-permute-start(bf16[128,256]{0,1:T(8,128)(2,1)S(1)} %bitcast.194), channel_id=1, source_target_pairs={{5,0},{6,1},{7,2},{8,3},{9,4},{10,5},{11,6},{12,7},{13,8},{14,9},{... | collective-permute-start | bytes 196616 | tf_op jit(solution)/shard_map/ppermute | solution.py:19
  48.1 15.2 %collective-permute-start.17 = (bf16[128,256]{0,1:T(8,128)(2,1)S(1)}, bf16[128,256]{0,1:T(8,128)(2,1)S(1)}, u32[]{:S(2)}, u32[]{:S(2)}) collective-permute-start(bf16[128,256]{0,1:T(8,128)(2,1)S(1)} %bitcast.195), channel_id=1, source_target_pairs={{6,0},{7,1},{8,2},{9,3},{10,4},{11,5},{12,6},{13,7},{14,8},{15,9},... | collective-permute-start | bytes 196616 | tf_op jit(solution)/shard_map/ppermute | solution.py:19
  50.1 16.8 %collective-permute-start.18 = (bf16[128,256]{0,1:T(8,128)(2,1)S(1)}, bf16[128,256]{0,1:T(8,128)(2,1)S(1)}, u32[]{:S(2)}, u32[]{:S(2)}) collective-permute-start(bf16[128,256]{0,1:T(8,128)(2,1)S(1)} %bitcast.196), channel_id=1, source_target_pairs={{7,0},{8,1},{9,2},{10,3},{11,4},{12,5},{13,6},{14,7},{15,8},{23,16... | collective-permute-start | bytes 196616 | tf_op jit(solution)/shard_map/ppermute | solution.py:19
  52.0 19.6 %collective-permute-start.19 = (bf16[128,256]{0,1:T(8,128)(2,1)S(1)}, bf16[128,256]{0,1:T(8,128)(2,1)S(1)}, u32[]{:S(2)}, u32[]{:S(2)}) collective-permute-start(bf16[128,256]{0,1:T(8,128)(2,1)S(1)} %bitcast.197), channel_id=1, source_target_pairs={{8,0},{9,1},{10,2},{11,3},{12,4},{13,5},{14,6},{15,7},{24,16},{25,... | collective-permute-start | bytes 196616 | tf_op jit(solution)/shard_map/ppermute | solution.py:19
  53.9 38.3 %collective-permute-start.1 = (bf16[512,256]{1,0:T(8,128)(2,1)S(1)}, bf16[512,256]{1,0:T(8,128)(2,1)}, u32[]{:S(2)}, u32[]{:S(2)}) collective-permute-start(bf16[512,256]{1,0:T(8,128)(2,1)S(1)} %fusion.53), channel_id=1, source_target_pairs={{0,2},{1,3},{2,4},{3,5},{4,6},{5,7},{6,8},{7,9},{8,10},{9,11},{10,... | collective-permute-start | bytes 786440 | tf_op jit(solution)/shard_map/ppermute | solution.py:19
  57.4 19.4 %collective-permute-start = (f32[512,64]{0,1:T(8,128)}, f32[512,64]{0,1:T(8,128)S(1)}, u32[]{:S(2)}, u32[]{:S(2)}) collective-permute-start(f32[512,64]{0,1:T(8,128)} %param.12), channel_id=1, source_target_pairs={{0,2},{1,3},{2,4},{3,5},{4,6},{5,7},{6,8},{7,9},{8,10},{9,11},{10,... | collective-permute-start | bytes 393224 | tf_op jit(solution)/shard_map/ppermute | solution.py:19
  63.4 31.3 %collective-permute-start.3 = (bf16[512,256]{1,0:T(8,128)(2,1)S(1)}, bf16[512,256]{1,0:T(8,128)(2,1)}, u32[]{:S(2)}, u32[]{:S(2)}) collective-permute-start(bf16[512,256]{1,0:T(8,128)(2,1)S(1)} %fusion.53), channel_id=1, source_target_pairs={{0,1},{1,2},{2,3},{3,4},{4,5},{5,6},{6,7},{7,8},{8,9},{9,10},{10,1... | collective-permute-start | bytes 786440 | tf_op jit(solution)/shard_map/ppermute | solution.py:19
  66.8 13.4 %collective-permute-start.2 = (f32[512,64]{0,1:T(8,128)}, f32[512,64]{0,1:T(8,128)}, u32[]{:S(2)}, u32[]{:S(2)}) collective-permute-start(f32[512,64]{0,1:T(8,128)} %param.12), channel_id=1, source_target_pairs={{0,1},{1,2},{2,3},{3,4},{4,5},{5,6},{6,7},{7,8},{8,9},{9,10},{10,1... | collective-permute-start | bytes 393224 | tf_op jit(solution)/shard_map/ppermute | solution.py:19
  71.6 21.9 %collective-permute-start.7 = (bf16[512,256]{1,0:T(8,128)(2,1)S(1)}, bf16[512,256]{1,0:T(8,128)(2,1)}, u32[]{:S(2)}, u32[]{:S(2)}) collective-permute-start(bf16[512,256]{1,0:T(8,128)(2,1)S(1)} %fusion.53), channel_id=1, source_target_pairs={{2,0},{3,1},{4,2},{5,3},{6,4},{7,5},{8,6},{9,7},{10,8},{11,9},{12,... | collective-permute-start | bytes 786440 | tf_op jit(solution)/shard_map/ppermute | solution.py:19
  75.5 0.9 copy-start.12
  76.7 1.4 copy-start.15
  76.7 9.1 %collective-permute-start.6 = (f32[512,64]{0,1:T(8,128)}, f32[512,64]{0,1:T(8,128)S(1)}, u32[]{:S(2)}, u32[]{:S(2)}) collective-permute-start(f32[512,64]{0,1:T(8,128)} %param.12), channel_id=1, source_target_pairs={{2,0},{3,1},{4,2},{5,3},{6,4},{7,5},{8,6},{9,7},{10,8},{11,9},{12,... | collective-permute-start | bytes 393224 | tf_op jit(solution)/shard_map/ppermute | solution.py:19
  80.2 12.0 %copy-start.4 = (bf16[512,512]{1,0:T(8,128)(2,1)}, bf16[512,512]{1,0:T(8,128)(2,1)S(1)}, u32[]{:S(2)}) copy-start(bf16[512,512]{1,0:T(8,128)(2,1)S(1)} %exponential_convert_fusion.3) | copy-start | bytes 1572868
  80.2 55.0 %collective-permute-start.5 = (bf16[512,256]{1,0:T(8,128)(2,1)S(1)}, bf16[512,256]{1,0:T(8,128)(2,1)}, u32[]{:S(2)}, u32[]{:S(2)}) collective-permute-start(bf16[512,256]{1,0:T(8,128)(2,1)S(1)} %fusion.53), channel_id=1, source_target_pairs={{1,0},{2,1},{3,2},{4,3},{5,4},{6,5},{7,6},{8,7},{9,8},{10,9},{11,1... | collective-permute-start | bytes 786440 | tf_op jit(solution)/shard_map/ppermute | solution.py:19
  84.6 10.2 %copy-start.2 = (bf16[512,512]{1,0:T(8,128)(2,1)}, bf16[512,512]{1,0:T(8,128)(2,1)S(1)}, u32[]{:S(2)}) copy-start(bf16[512,512]{1,0:T(8,128)(2,1)S(1)} %exponential_convert_fusion.2) | copy-start | bytes 1572868
  85.8 3.4 %collective-permute-start.4 = (f32[512,64]{0,1:T(8,128)}, f32[512,64]{0,1:T(8,128)S(1)}, u32[]{:S(2)}, u32[]{:S(2)}) collective-permute-start(f32[512,64]{0,1:T(8,128)} %param.12), channel_id=1, source_target_pairs={{1,0},{2,1},{3,2},{4,3},{5,4},{6,5},{7,6},{8,7},{9,8},{10,9},{11,1... | collective-permute-start | bytes 393224 | tf_op jit(solution)/shard_map/ppermute | solution.py:19
  102.8 28.1 %copy-start.7 = (bf16[1,128,128]{2,1,0:T(8,128)(2,1)S(1)}, bf16[1,128,128]{2,1,0:T(8,128)(2,1)}, u32[]{:S(2)}) copy-start(bf16[1,128,128]{2,1,0:T(8,128)(2,1)} %param.18) | copy-start | bytes 98308
  132.2 2.9 %copy-start.10 = (f32[512,256]{1,0:T(8,128)S(1)}, f32[512,256]{1,0:T(8,128)}, u32[]{:S(2)}) copy-start(f32[512,256]{1,0:T(8,128)} %param.13) | copy-start | bytes 1572868
  137.9 50.9 %collective-permute-start.20 = (bf16[512,256]{1,0:T(8,128)(2,1)S(1)}, bf16[512,256]{1,0:T(8,128)(2,1)}, u32[]{:S(2)}, u32[]{:S(2)}) collective-permute-start(bf16[512,256]{1,0:T(8,128)(2,1)S(1)} %get-tuple-element.18), channel_id=1, source_target_pairs={{0,2},{1,3},{2,4},{3,5},{4,6},{5,7},{6,8},{7,9},{8,10},{9,11},{10,... | collective-permute-start | bytes 786440 | tf_op jit(solution)/shard_map/ppermute | solution.py:19
  139.9 52.3 %collective-permute-start.21 = (bf16[512,256]{1,0:T(8,128)(2,1)S(1)}, bf16[512,256]{1,0:T(8,128)(2,1)}, u32[]{:S(2)}, u32[]{:S(2)}) collective-permute-start(bf16[512,256]{1,0:T(8,128)(2,1)S(1)} %get-tuple-element.18), channel_id=1, source_target_pairs={{0,1},{1,2},{2,3},{3,4},{4,5},{5,6},{6,7},{7,8},{8,9},{9,10},{10,1... | collective-permute-start | bytes 786440 | tf_op jit(solution)/shard_map/ppermute | solution.py:19
  144.8 5.2 %copy-start.8 = (bf16[1,128,128]{2,1,0:T(8,128)(2,1)S(1)}, bf16[1,128,128]{2,1,0:T(8,128)(2,1)}, u32[]{:S(2)}) copy-start(bf16[1,128,128]{2,1,0:T(8,128)(2,1)} %param.18) | copy-start | bytes 98308
  145.1 5.0 %copy-start.19 = (f32[4]{0:T(128)S(1)}, f32[4]{0:T(128)}, u32[]{:S(2)}) copy-start(f32[4]{0:T(128)} %copy-done.18) | copy-start | bytes 52
  145.1 6.0 %collective-permute-start.24 = (bf16[128,256]{0,1:T(8,128)(2,1)S(1)}, bf16[128,256]{0,1:T(8,128)(2,1)S(1)}, u32[]{:S(2)}, u32[]{:S(2)}) collective-permute-start(bf16[128,256]{0,1:T(8,128)(2,1)S(1)} %bitcast.198), channel_id=1, source_target_pairs={{0,8},{1,9},{2,10},{3,11},{4,12},{5,13},{6,14},{7,15},{16,24},{17,... | collective-permute-start | bytes 196616 | tf_op jit(solution)/shard_map/ppermute | solution.py:19
  146.4 7.1 %collective-permute-start.25 = (bf16[128,256]{0,1:T(8,128)(2,1)S(1)}, bf16[128,256]{0,1:T(8,128)(2,1)S(1)}, u32[]{:S(2)}, u32[]{:S(2)}) collective-permute-start(bf16[128,256]{0,1:T(8,128)(2,1)S(1)} %bitcast.199), channel_id=1, source_target_pairs={{0,7},{1,8},{2,9},{3,10},{4,11},{5,12},{6,13},{7,14},{8,15},{16,23... | collective-permute-start | bytes 196616 | tf_op jit(solution)/shard_map/ppermute | solution.py:19
  147.7 8.8 %collective-permute-start.26 = (bf16[128,256]{0,1:T(8,128)(2,1)S(1)}, bf16[128,256]{0,1:T(8,128)(2,1)S(1)}, u32[]{:S(2)}, u32[]{:S(2)}) collective-permute-start(bf16[128,256]{0,1:T(8,128)(2,1)S(1)} %bitcast.200), channel_id=1, source_target_pairs={{0,6},{1,7},{2,8},{3,9},{4,10},{5,11},{6,12},{7,13},{8,14},{9,15},... | collective-permute-start | bytes 196616 | tf_op jit(solution)/shard_map/ppermute | solution.py:19
  151.1 9.0 %collective-permute-start.27 = (bf16[128,256]{0,1:T(8,128)(2,1)S(1)}, bf16[128,256]{0,1:T(8,128)(2,1)S(1)}, u32[]{:S(2)}, u32[]{:S(2)}) collective-permute-start(bf16[128,256]{0,1:T(8,128)(2,1)S(1)} %bitcast.201), channel_id=1, source_target_pairs={{0,5},{1,6},{2,7},{3,8},{4,9},{5,10},{6,11},{7,12},{8,13},{9,14},{... | collective-permute-start | bytes 196616 | tf_op jit(solution)/shard_map/ppermute | solution.py:19
  153.5 8.5 %collective-permute-start.28 = (bf16[128,256]{0,1:T(8,128)(2,1)S(1)}, bf16[128,256]{0,1:T(8,128)(2,1)S(1)}, u32[]{:S(2)}, u32[]{:S(2)}) collective-permute-start(bf16[128,256]{0,1:T(8,128)(2,1)S(1)} %bitcast.202), channel_id=1, source_target_pairs={{0,4},{1,5},{2,6},{3,7},{4,8},{5,9},{6,10},{7,11},{8,12},{9,13},{1... | collective-permute-start | bytes 196616 | tf_op jit(solution)/shard_map/ppermute | solution.py:19
  156.5 7.5 %collective-permute-start.29 = (bf16[128,256]{0,1:T(8,128)(2,1)S(1)}, bf16[128,256]{0,1:T(8,128)(2,1)S(1)}, u32[]{:S(2)}, u32[]{:S(2)}) collective-permute-start(bf16[128,256]{0,1:T(8,128)(2,1)S(1)} %bitcast.203), channel_id=1, source_target_pairs={{0,3},{1,4},{2,5},{3,6},{4,7},{5,8},{6,9},{7,10},{8,11},{9,12},{10... | collective-permute-start | bytes 196616 | tf_op jit(solution)/shard_map/ppermute | solution.py:19
  160.1 5.8 %collective-permute-start.30 = (bf16[128,256]{0,1:T(8,128)(2,1)S(1)}, bf16[128,256]{0,1:T(8,128)(2,1)S(1)}, u32[]{:S(2)}, u32[]{:S(2)}) collective-permute-start(bf16[128,256]{0,1:T(8,128)(2,1)S(1)} %bitcast.204), channel_id=1, source_target_pairs={{3,0},{4,1},{5,2},{6,3},{7,4},{8,5},{9,6},{10,7},{11,8},{12,9},{13... | collective-permute-start | bytes 196616 | tf_op jit(solution)/shard_map/ppermute | solution.py:19
  162.1 6.8 %collective-permute-start.31 = (bf16[128,256]{0,1:T(8,128)(2,1)S(1)}, bf16[128,256]{0,1:T(8,128)(2,1)S(1)}, u32[]{:S(2)}, u32[]{:S(2)}) collective-permute-start(bf16[128,256]{0,1:T(8,128)(2,1)S(1)} %bitcast.205), channel_id=1, source_target_pairs={{4,0},{5,1},{6,2},{7,3},{8,4},{9,5},{10,6},{11,7},{12,8},{13,9},{1... | collective-permute-start | bytes 196616 | tf_op jit(solution)/shard_map/ppermute | solution.py:19
  164.0 7.6 %collective-permute-start.32 = (bf16[128,256]{0,1:T(8,128)(2,1)S(1)}, bf16[128,256]{0,1:T(8,128)(2,1)S(1)}, u32[]{:S(2)}, u32[]{:S(2)}) collective-permute-start(bf16[128,256]{0,1:T(8,128)(2,1)S(1)} %bitcast.206), channel_id=1, source_target_pairs={{5,0},{6,1},{7,2},{8,3},{9,4},{10,5},{11,6},{12,7},{13,8},{14,9},{... | collective-permute-start | bytes 196616 | tf_op jit(solution)/shard_map/ppermute | solution.py:19
  165.9 9.6 %collective-permute-start.33 = (bf16[128,256]{0,1:T(8,128)(2,1)S(1)}, bf16[128,256]{0,1:T(8,128)(2,1)S(1)}, u32[]{:S(2)}, u32[]{:S(2)}) collective-permute-start(bf16[128,256]{0,1:T(8,128)(2,1)S(1)} %bitcast.207), channel_id=1, source_target_pairs={{6,0},{7,1},{8,2},{9,3},{10,4},{11,5},{12,6},{13,7},{14,8},{15,9},... | collective-permute-start | bytes 196616 | tf_op jit(solution)/shard_map/ppermute | solution.py:19
  168.8 8.5 %collective-permute-start.34 = (bf16[128,256]{0,1:T(8,128)(2,1)S(1)}, bf16[128,256]{0,1:T(8,128)(2,1)S(1)}, u32[]{:S(2)}, u32[]{:S(2)}) collective-permute-start(bf16[128,256]{0,1:T(8,128)(2,1)S(1)} %bitcast.208), channel_id=1, source_target_pairs={{7,0},{8,1},{9,2},{10,3},{11,4},{12,5},{13,6},{14,7},{15,8},{23,16... | collective-permute-start | bytes 196616 | tf_op jit(solution)/shard_map/ppermute | solution.py:19
  171.5 13.5 %collective-permute-start.35 = (bf16[128,256]{0,1:T(8,128)(2,1)S(1)}, bf16[128,256]{0,1:T(8,128)(2,1)S(1)}, u32[]{:S(2)}, u32[]{:S(2)}) collective-permute-start(bf16[128,256]{0,1:T(8,128)(2,1)S(1)} %bitcast.209), channel_id=1, source_target_pairs={{8,0},{9,1},{10,2},{11,3},{12,4},{13,5},{14,6},{15,7},{24,16},{25,... | collective-permute-start | bytes 196616 | tf_op jit(solution)/shard_map/ppermute | solution.py:19
  175.5 15.5 %collective-permute-start.23 = (bf16[512,256]{1,0:T(8,128)(2,1)S(1)}, bf16[512,256]{1,0:T(8,128)(2,1)}, u32[]{:S(2)}, u32[]{:S(2)}) collective-permute-start(bf16[512,256]{1,0:T(8,128)(2,1)S(1)} %get-tuple-element.18), channel_id=1, source_target_pairs={{2,0},{3,1},{4,2},{5,3},{6,4},{7,5},{8,6},{9,7},{10,8},{11,9},{12,... | collective-permute-start | bytes 786440 | tf_op jit(solution)/shard_map/ppermute | solution.py:19
  177.4 57.0 %collective-permute-start.22 = (bf16[512,256]{1,0:T(8,128)(2,1)S(1)}, bf16[512,256]{1,0:T(8,128)(2,1)}, u32[]{:S(2)}, u32[]{:S(2)}) collective-permute-start(bf16[512,256]{1,0:T(8,128)(2,1)S(1)} %get-tuple-element.18), channel_id=1, source_target_pairs={{1,0},{2,1},{3,2},{4,3},{5,4},{6,5},{7,6},{8,7},{9,8},{10,9},{11,1... | collective-permute-start | bytes 786440 | tf_op jit(solution)/shard_map/ppermute | solution.py:19
  187.7 0.9 copy-start.13
  188.6 1.0 copy-start.5
  190.9 1.3 copy-start.3
  211.2 20.3 %copy-start.9 = (bf16[1,128,128]{2,1,0:T(8,128)(2,1)S(1)}, bf16[1,128,128]{2,1,0:T(8,128)(2,1)}, u32[]{:S(2)}) copy-start(bf16[1,128,128]{2,1,0:T(8,128)(2,1)} %param.18) | copy-start | bytes 98308
  232.0 2.4 copy-start.11
Sparse Core Ops, SparseCore 0:
  28.5 57.2 reduce-scatter.2
  151.2 53.9 reduce-scatter.4
where the time goes:
time: 246 us; the launch traced here: 244 us
  starting transfers between devices  72.8 us (30%)
  blocking collectives  57.2 us (23%)
  local copies, waits for them, and re-layouts  36.7 us (15%)
  matrix products  28.5 us (12%)
  waiting for transfers between devices  22.6 us (9%)
  between operations  19 us (8%)
  other arithmetic  7.11 us (3%)
    ppermute x36, starting transfers between devices, from_behind(): return lax.ppermute(shard, axis, pairs)  72.7 us
    all_gather x2, blocking collectives, operate(): whole_columns = lax.all_gather(partial_coupled, 'dev', axis=2, tiled=True)  48.4 us
    unnamed x66, local copies, waits for them, and re-layouts  18.5 us
    dot_general x8, matrix products, operate(): jnp.dot(block_here, remote, preferred_element_type=jnp.float32)  13.5 us
    reduce_scatter x2, waiting for transfers between devices, operate(): lax.psum_scatter(contrib, 'dev', scatter_dimension=2, tiled=True)  11.7 us
    dot_general x5, matrix products, kernel_block(): jnp.dot(left_points, right_points.T, precision=lax.Precision.HIGHEST, pre...  11.4 us
    ppermute x36, waiting for transfers between devices, from_behind(): return lax.ppermute(shard, axis, pairs)  10.9 us
    all_gather x2, blocking collectives, operate(): every_column = lax.all_gather(column_sums, 'grp', axis=0, tiled=True)  8.79 us
  transfers between devices with their start and end apart: 38, of which 6 were waited for; matrix products, arithmetic and copies ran while one was open for 24% of the time, Pallas kernels for 0%

commit v1 on v0

--- a/solution.py
+++ b/solution.py
@@ -1,7 +1,13 @@
+import functools
+
 import jax
 import jax.numpy as jnp
 from jax import lax
+from jax.experimental import pallas as pl
+from jax.experimental.pallas import tpu as pltpu
 from jax.sharding import PartitionSpec as P
+
+MESH = pl.DeviceIdType.MESH
 
 REACH = 2
 FARREACH = 8
@@ -134,7 +140,394 @@
     return (solution, residual)
 
 
+def fused_kernel(
+    n,
+    coords_ref,
+    right_ref,
+    perm_ref,
+    near_ref,
+    far_ref,
+    coup_ref,
+    transfer_ref,
+    basis_ref,
+    cluster_ref,
+    farclus_ref,
+    cluscoup_ref,
+    ridge_ref,
+    sol_ref,
+    res_ref,
+    points,
+    wide,
+    blocks,
+    skel,
+    moved,
+    spread_t,
+    chosen,
+    mine,
+    theirs,
+    coup_out,
+    coup_in,
+    basis_p,
+    basis_t,
+    acc,
+    direction,
+    near_send,
+    near_recv,
+    tree_send,
+    tree_recv,
+    mate_send,
+    mate_recv,
+    grp_send,
+    grp_recv,
+):
+    f32, bf16 = jnp.float32, jnp.bfloat16
+    group = lax.axis_index("grp")
+    me = lax.axis_index("dev")
+    other = 1 - group
+    chips = n // 2
+    chip = lax.div(me, 2)
+    core = lax.rem(me, 2)
+    row = lax.rem(chip, 2)
+    mate = chip * 2 + (1 - core)
+    across = me + 2 - 4 * row
+    leaf, outs = right_ref.shape
+    rank = transfer_ref.shape[1]
+    clusters = cluscoup_ref.shape[0]
+    has_z = ((row == 0) & (me >= 4)) | ((row == 1) & (me + 4 < n))
+    sends_z = ((row == 0) & (me + 4 < n)) | ((row == 1) & (me >= 4))
+    z_target = jnp.where(sends_z, me + 4 - 8 * row, me)
+
+    barrier = pltpu.get_barrier_semaphore()
+    for step in range(1, n):
+        pl.semaphore_signal(
+            barrier, inc=1, device_id={"dev": lax.rem(me + step, n)}, device_id_type=MESH
+        )
+    pl.semaphore_signal(barrier, inc=1, device_id={"grp": other}, device_id_type=MESH)
+
+    def near_copy(buf, stage, source, slot, target, size):
+        return pltpu.make_async_remote_copy(
+            src_ref=buf.at[pl.ds(source * size, size)],
+            dst_ref=buf.at[pl.ds(slot * size, size)],
+            send_sem=near_send.at[stage, slot],
+            recv_sem=near_recv.at[stage, slot],
+            device_id={"dev": target},
+            device_id_type=MESH,
+        )
+
+    def near_start(buf, stage, size):
+        near_copy(buf, stage, 0, 2, across, size).start()
+        near_copy(buf, stage, 0, 1, mate, size).start()
+
+        @pl.when(jnp.logical_not(has_z))
+        def _():
+            buf[pl.ds(3 * size, size), :] = jnp.zeros((size, buf.shape[1]), buf.dtype)
+
+        @pl.when(jnp.logical_not(has_z) & (core == row))
+        def _():
+            buf[pl.ds(4 * size, size), :] = jnp.zeros((size, buf.shape[1]), buf.dtype)
+
+    def near_relay(buf, stage, size):
+        near_copy(buf, stage, 0, 2, across, size).wait_recv()
+
+        @pl.when(sends_z)
+        def _():
+            near_copy(buf, stage, 2, 3, z_target, size).start()
+
+        @pl.when(core == row)
+        def _():
+            near_copy(buf, stage, 2, 4, mate, size).start()
+
+        @pl.when(has_z)
+        def _():
+            near_copy(buf, stage, 2, 3, mate, size).wait_recv()
+
+        @pl.when(has_z & (core != row))
+        def _():
+            near_copy(buf, stage, 3, 4, mate, size).start()
+
+    def near_finish(buf, stage, size):
+        near_copy(buf, stage, 0, 1, mate, size).wait_recv()
+
+        @pl.when(has_z | (core != row))
+        def _():
+            near_copy(buf, stage, 0, 4, mate, size).wait_recv()
+
+    def near_drain(buf, stage, size):
+        near_copy(buf, stage, 0, 1, mate, size).wait_send()
+        near_copy(buf, stage, 0, 2, across, size).wait_send()
+
+        @pl.when(sends_z)
+        def _():
+            near_copy(buf, stage, 2, 3, z_target, size).wait_send()
+
+        @pl.when(has_z | (core == row))
+        def _():
+            near_copy(buf, stage, 0, 4, mate, size).wait_send()
+
+    def tree_block(buf, owner, size):
+        return buf.at[pl.ds(pl.multiple_of(owner * size, 16), size)]
+
+    def tree_copy(buf, stage, step, owner, target, size, send, recv):
+        return pltpu.make_async_remote_copy(
+            src_ref=tree_block(buf, owner, size),
+            dst_ref=tree_block(buf, owner, size),
+            send_sem=send.at[stage, step],
+            recv_sem=recv.at[stage, step],
+            device_id={"dev": target},
+            device_id_type=MESH,
+        )
+
+    def same_core(step):
+        return lax.rem(chip + step + chips, chips) * 2 + core
+
+    def tree_start(buf, stage, size):
+        for step in range(1, chips):
+            tree_copy(buf, stage, step, me, same_core(step), size, tree_send, tree_recv).start()
+        tree_copy(buf, stage, 0, me, mate, size, mate_send, mate_recv).start()
+
+    def tree_relay(buf, stage, size):
+        for step in range(1, chips):
+            owner = same_core(-step)
+            tree_copy(buf, stage, step, owner, mate, size, tree_send, tree_recv).wait_recv()
+            tree_copy(buf, stage, step, owner, mate, size, mate_send, mate_recv).start()
+
+    def tree_finish(buf, stage, size):
+        for step in range(chips):
+            owner = lax.rem(chip - step + chips, chips) * 2 + (1 - core)
+            tree_copy(buf, stage, step, owner, mate, size, mate_send, mate_recv).wait_recv()
+
+    def tree_drain(buf, stage, size):
+        for step in range(chips):
+            tree_copy(buf, stage, step, me, mate, size, mate_send, mate_recv).wait_send()
+            if step > 0:
+                tree_copy(buf, stage, step, me, mate, size, tree_send, tree_recv).wait_send()
+
+    def grp_copy(source, target, stage):
+        return pltpu.make_async_remote_copy(
+            src_ref=source,
+            dst_ref=target,
+            send_sem=grp_send.at[stage],
+            recv_sem=grp_recv.at[stage],
+            device_id={"grp": other},
+            device_id_type=MESH,
+        )
+
+    points[pl.ds(0, leaf), :] = coords_ref[...]
+    transfer_rows = transfer_ref[0]
+    packed = rank + 16
+    local_cluster = jnp.clip(cluster_ref[0] - group * clusters, 0, clusters - 1)
+    lane_rows = lax.broadcasted_iota(jnp.int32, (16, rank), 0)
+    tags = jnp.where(lane_rows == local_cluster, 1.0, 0.0).astype(bf16)
+    own_rows = pl.multiple_of(me * packed, 16)
+    moved[pl.ds(own_rows, rank), :] = transfer_rows.astype(f32).T.astype(bf16)
+    moved[pl.ds(own_rows + rank, 16), :] = tags
+    for place in range(clusters):
+        total = jnp.zeros((rank, rank), f32)
+        for k in range(farclus_ref.shape[1]):
+            hit = (farclus_ref[local_cluster, k] == other * clusters + place).astype(f32)
+            total = total + hit * cluscoup_ref[local_cluster, k].astype(f32)
+        mine[:, place * rank : (place + 1) * rank] = total.astype(bf16)
+
+    pl.semaphore_wait(barrier, n)
+    near_start(points, 0, leaf)
+    tree_start(moved, 0, packed)
+    grp_copy(mine, theirs, 0).start()
+
+    targets = lax.broadcasted_iota(jnp.int32, (leaf, leaf), 0)
+    one_hot = jnp.where(targets == perm_ref[...], 1.0, 0.0).astype(bf16)
+    placed = jnp.dot(one_hot, basis_ref[...], preferred_element_type=f32)
+    basis_p[...] = placed.astype(bf16)
+    basis_t[...] = placed.T.astype(bf16)
+    for place in range(n):
+        total = jnp.zeros((rank, rank), f32)
+        for k in range(far_ref.shape[1]):
+            hit = (far_ref[0, k] == group * n + place).astype(f32)
+            total = total + hit * coup_ref[0, k].astype(f32)
+        chosen[:, place * rank : (place + 1) * rank] = total.astype(bf16)
+
+    last = (((1,), (1,)), ((), ()))
+    left = coords_ref[...]
+    left_sq = jnp.sum(left * left, axis=1, keepdims=True)
+
+    def fill_block(slot, source):
+        right = points[pl.ds(slot * leaf, leaf), :]
+        right_sq = lax.dot_general(
+            jnp.ones((8, right.shape[1]), f32),
+            right * right,
+            last,
+            precision=lax.Precision.HIGHEST,
+            preferred_element_type=f32,
+        )[0:1, :]
+        inner = lax.dot_general(
+            left, right, last, precision=lax.Precision.HIGHEST, preferred_element_type=f32
+        )
+        block = jnp.exp(-kernel_scale * (left_sq + right_sq - 2.0 * inner))
+        if source is not None:
+            wanted = group * n + source
+            hit = jnp.float32(0.0)
+            for k in range(near_ref.shape[1]):
+                listed = (near_ref[0, k] == wanted) & (near_ref[0, k] >= 0)
+                hit = hit + listed.astype(f32)
+            block = hit * block
+        blocks[:, slot * leaf : (slot + 1) * leaf] = block.astype(bf16)
+
+    ridge = ridge_ref[...]
+    bottom_edge = ridge + spectrum_gap
+    top_edge = ridge + spectrum_top
+    centre = (top_edge + bottom_edge) / 2.0
+    spread = (top_edge - bottom_edge) / 2.0
+    sigma_ratio = centre / spread
+    contraction = 1.0 / sigma_ratio
+    start = right_ref[...] / centre
+    direction[...] = start
+    sol_ref[...] = start
+    res_ref[...] = right_ref[...]
+
+    def launch(rounds):
+        values = direction[...].astype(bf16)
+        wide[rounds, pl.ds(0, leaf), :] = values
+        skeleton = jnp.dot(basis_t[...], values, preferred_element_type=f32).astype(bf16)
+        skel[rounds, pl.ds(pl.multiple_of(me * rank, 16), rank), :] = skeleton
+        tree_start(skel.at[rounds], rounds + 1, rank)
+        near_start(wide.at[rounds], rounds + 1, leaf)
+
+    fill_block(0, None)
+    tree_relay(moved, 0, packed)
+    near_relay(points, 0, leaf)
+    launch(0)
+    near_finish(points, 0, leaf)
+    fill_block(1, mate)
+    fill_block(2, across)
+    tree_finish(moved, 0, packed)
+    for place in range(n):
+        part = moved[place * packed : place * packed + rank, :]
+        for c in range(clusters):
+            tag = moved[place * packed + rank : place * packed + packed, :][c : c + 1, :]
+            spread_t[c * rank : (c + 1) * rank, place * rank : (place + 1) * rank] = (
+                part.astype(f32) * tag.astype(f32)
+            ).astype(bf16)
+
+    for rounds in range(ITERS):
+        stage = rounds + 1
+        if rounds > 0:
+            launch(rounds)
+        acc[...] = ridge * direction[...] + jnp.dot(
+            blocks[:, 0:leaf], wide[rounds, 0:leaf, :], preferred_element_type=f32
+        )
+        tree_relay(skel.at[rounds], stage, rank)
+        near_relay(wide.at[rounds], stage, leaf)
+        if rounds == 0:
+            fill_block(3, me - 2 + 4 * row)
+            fill_block(4, me - 1 + 2 * core)
+            grp_copy(mine, theirs, 0).wait_recv()
+        tree_finish(skel.at[rounds], stage, rank)
+        sums = jnp.dot(spread_t[...], skel[rounds], preferred_element_type=f32).astype(bf16)
+        coup_out[rounds] = jnp.dot(theirs[...], sums, preferred_element_type=f32).astype(bf16)
+        grp_copy(coup_out.at[rounds], coup_in.at[rounds], stage).start()
+        level_one = jnp.dot(chosen[...], skel[rounds], preferred_element_type=f32)
+        near_finish(wide.at[rounds], stage, leaf)
+        acc[...] += jnp.dot(
+            blocks[:, leaf:], wide[rounds, leaf:, :], preferred_element_type=f32
+        )
+        grp_copy(coup_out.at[rounds], coup_in.at[rounds], stage).wait_recv()
+        down = jnp.dot(transfer_rows, coup_in[rounds], preferred_element_type=f32)
+        far_part = jnp.dot(
+            basis_p[...], (level_one + down).astype(bf16), preferred_element_type=f32
+        )
+        residual = res_ref[...] - (acc[...] + far_part)
+        res_ref[...] = residual
+        rho_next = 1.0 / (2.0 * sigma_ratio - contraction)
+        moved_on = rho_next * contraction * direction[...] + 2.0 * rho_next / spread * residual
+        direction[...] = moved_on
+        sol_ref[...] += moved_on
+        contraction = rho_next
+
+    near_drain(points, 0, leaf)
+    tree_drain(moved, 0, packed)
+    grp_copy(mine, theirs, 0).wait_send()
+    for rounds in range(ITERS):
+        near_drain(wide.at[rounds], rounds + 1, leaf)
+        tree_drain(skel.at[rounds], rounds + 1, rank)
+        grp_copy(coup_out.at[rounds], coup_in.at[rounds], rounds + 1).wait_send()
+
+
+def fused_body(
+    coords,
+    right_side,
+    leaf_perm,
+    near_list,
+    far_leaves,
+    couplings,
+    transfer,
+    leaf_basis,
+    cluster_of,
+    far_clusters,
+    cluster_couplings,
+    ridge_weight,
+):
+    n = lax.axis_size("dev")
+    leaf, dim = coords.shape
+    outs = right_side.shape[1]
+    rank = transfer.shape[1]
+    clusters = cluster_couplings.shape[0]
+    bf16, f32 = jnp.bfloat16, jnp.float32
+    vmem = pl.BlockSpec(memory_space=pltpu.VMEM)
+    smem = pl.BlockSpec(memory_space=pltpu.SMEM)
+    sem = pltpu.SemaphoreType.DMA
+    stages = ITERS + 1
+    out = jax.ShapeDtypeStruct((leaf, outs), f32)
+    return pl.pallas_call(
+        functools.partial(fused_kernel, n),
+        out_shape=(out, out),
+        in_specs=[vmem, vmem, vmem, smem, smem, vmem, vmem, vmem, smem, smem, vmem, vmem],
+        out_specs=(vmem, vmem),
+        scratch_shapes=[
+            pltpu.VMEM((5 * leaf, dim), f32),
+            pltpu.VMEM((ITERS, 5 * leaf, outs), bf16),
+            pltpu.VMEM((leaf, 5 * leaf), bf16),
+            pltpu.VMEM((ITERS, n * rank, outs), bf16),
+            pltpu.VMEM((n * (rank + 16), rank), bf16),
+            pltpu.VMEM((clusters * rank, n * rank), bf16),
+            pltpu.VMEM((rank, n * rank), bf16),
+            pltpu.VMEM((rank, clusters * rank), bf16),
+            pltpu.VMEM((rank, clusters * rank), bf16),
+            pltpu.VMEM((ITERS, rank, outs), bf16),
+            pltpu.VMEM((ITERS, rank, outs), bf16),
+            pltpu.VMEM((leaf, rank), bf16),
+            pltpu.VMEM((rank, leaf), bf16),
+            pltpu.VMEM((leaf, outs), f32),
+            pltpu.VMEM((leaf, outs), f32),
+            sem((stages, 5)),
+            sem((stages, 5)),
+            sem((stages, n // 2)),
+            sem((stages, n // 2)),
+            sem((stages, n // 2)),
+            sem((stages, n // 2)),
+            sem((stages,)),
+            sem((stages,)),
+        ],
+        compiler_params=pltpu.CompilerParams(
+            collective_id=0, has_side_effects=True, vmem_limit_bytes=48 << 20
+        ),
+        name="fused_solve",
+    )(
+        coords,
+        right_side,
+        leaf_perm,
+        near_list,
+        far_leaves,
+        couplings,
+        transfer,
+        leaf_basis,
+        cluster_of,
+        far_clusters,
+        cluster_couplings,
+        ridge_weight.reshape(1, 1),
+    )
+
+
 def solution(mesh):
+    fits = mesh.shape["grp"] == 2 and mesh.shape["dev"] % 4 == 0
     placed = (
         P(("grp", "dev"), None),
         P(("grp", "dev"), None),
@@ -150,7 +543,7 @@
         P(),
     )
     return jax.shard_map(
-        body,
+        fused_body if fits else body,
         mesh=mesh,
         in_specs=placed,
         out_specs=(P(("grp", "dev"), None), P(("grp", "dev"), None)),

time: 246 us -> 81 us (0.33)
  the two profiles are of different devices: /device:TPU:0 before, /device:TPU:4 now
where the time goes in v1:
time: 81 us; the launch traced here: 80.6 us
  Pallas kernels  73.7 us (91%)
  local copies, waits for them, and re-layouts  4.86 us (6%)
  between operations  2.06 us (3%)
    pallas_call x1, Pallas kernels, fused_body(): pl.pallas_call(functools.partial(fused_kernel, n), out_shape=(out, out),...  73.7 us
    unnamed x21, local copies, waits for them, and re-layouts  4.86 us

profile of v1, /device:TPU:4, one launch (start us, length us, event | category | flops | bytes accessed | tf_op | source)
XLA Modules:
  0.0 80.6 jit_solution(11965880920489006885)
XLA Ops:
  1.9 0.0 copy-start.2
  1.9 0.0 copy-start.3
  1.9 0.0 copy-start.4
  2.0 0.0 copy-start.5
  2.0 0.0 copy-start.6
  2.0 0.0 copy-start.7
  2.0 0.0 copy-start.8
  2.0 1.2 %copy.14.coords_ref = f32[512,64]{1,0:T(8,128)S(1)} copy(f32[512,64]{0,1:T(8,128)} %param.12) | data formatting | bytes 262144 | tf_op args[0]
  3.2 0.0 copy-done.2
  3.2 0.0 copy-done.3
  3.2 0.0 copy-done.4
  3.2 0.0 copy-done.5
  3.2 0.0 copy-done.6
  3.2 0.0 copy-done.7
  3.2 0.0 copy-done.8
  3.2 0.0 copy-start
  3.2 1.0 %copy-done = f32[512,256]{1,0:T(8,128)S(1)} copy-done((f32[512,256]{1,0:T(8,128)S(1)}, f32[512,256]{1,0:T(8,128)}, u32[]{:S(2)}) %copy-start) | copy-done | bytes 524312
  4.3 0.0 copy-start.1
  4.3 1.0 %copy-done.1 = bf16[4,4,128,128]{3,2,1,0:T(8,128)(2,1)S(1)} copy-done((bf16[4,4,128,128]{3,2,1,0:T(8,128)(2,1)S(1)}, bf16[4,4,128,128]{3,2,1,0:T(8,128)(2,1)}, u32[]{:S(2)}) %copy-start.1) | copy-done | bytes 524312
  5.3 73.7 %fused_solve.1 = (f32[512,256]{1,0:T(8,128)S(1)}, f32[512,256]{1,0:T(8,128)S(1)}) custom-call(f32[512,64]{1,0:T(8,128)S(1)} %copy.14.coords_ref, f32[512,256]{1,0:T(8,128)S(1)} %copy-done, s32[1,512]{1,0:T(1,128)S(1)} %copy-done.5, s32[1,4]{1,0:T(1,128)S(1)} %copy-done.7, s32[1,4]{1,0:T(1,128)S(1)} %copy-done.8, bf16[1,4,128,128]{3,2,1,0:T(8,128)(2,1)S(1)} %copy-done.2, ...), custom_call_target="tpu_custom_call" | custom-call | tf_op jit(solution)/shard_map/fused_solve/pallas_call | solution.py:479
  79.1 0.8 copy.19
  79.9 0.8 copy.20
Async XLA Ops:
  1.9 1.2 %copy-start.2 = (bf16[1,4,128,128]{3,2,1,0:T(8,128)(2,1)S(1)}, bf16[1,4,128,128]{3,2,1,0:T(8,128)(2,1)}, u32[]{:S(2)}) copy-start(bf16[1,4,128,128]{3,2,1,0:T(8,128)(2,1)} %coup_ref.1) | copy-start | bytes 393220
  1.9 1.2 %copy-start.3 = (bf16[512,128]{1,0:T(8,128)(2,1)S(1)}, bf16[512,128]{1,0:T(8,128)(2,1)}, u32[]{:S(2)}) copy-start(bf16[512,128]{1,0:T(8,128)(2,1)} %basis_ref.1) | copy-start | bytes 393220
  1.9 1.2 %copy-start.4 = (bf16[1,128,128]{2,1,0:T(8,128)(2,1)S(1)}, bf16[1,128,128]{2,1,0:T(8,128)(2,1)}, u32[]{:S(2)}) copy-start(bf16[1,128,128]{2,1,0:T(8,128)(2,1)} %transfer_ref.1) | copy-start | bytes 98308
  2.0 1.2 %copy-start.5 = (s32[1,512]{1,0:T(1,128)S(1)}, s32[1,512]{1,0:T(1,128)}, u32[]{:S(2)}) copy-start(s32[1,512]{1,0:T(1,128)} %perm_ref.1) | copy-start | bytes 6148
  2.0 1.2 %copy-start.6 = (s32[4,4]{1,0:T(4,128)S(1)}, s32[4,4]{1,0:T(4,128)}, u32[]{:S(2)}) copy-start(s32[4,4]{1,0:T(4,128)} %farclus_ref.1) | copy-start | bytes 196
  2.0 1.2 %copy-start.7 = (s32[1,4]{1,0:T(1,128)S(1)}, s32[1,4]{1,0:T(1,128)}, u32[]{:S(2)}) copy-start(s32[1,4]{1,0:T(1,128)} %near_ref.1) | copy-start | bytes 52
  2.0 1.2 %copy-start.8 = (s32[1,4]{1,0:T(1,128)S(1)}, s32[1,4]{1,0:T(1,128)}, u32[]{:S(2)}) copy-start(s32[1,4]{1,0:T(1,128)} %far_ref.1) | copy-start | bytes 52
  3.2 1.0 %copy-start = (f32[512,256]{1,0:T(8,128)S(1)}, f32[512,256]{1,0:T(8,128)}, u32[]{:S(2)}) copy-start(f32[512,256]{1,0:T(8,128)} %right_ref.1) | copy-start | bytes 1572868
  4.3 1.0 %copy-start.1 = (bf16[4,4,128,128]{3,2,1,0:T(8,128)(2,1)S(1)}, bf16[4,4,128,128]{3,2,1,0:T(8,128)(2,1)}, u32[]{:S(2)}) copy-start(bf16[4,4,128,128]{3,2,1,0:T(8,128)(2,1)} %cluscoup_ref.1) | copy-start | bytes 1572868

commit v2 on v1

--- a/solution.py
+++ b/solution.py
@@ -8,6 +8,7 @@
 from jax.sharding import PartitionSpec as P
 
 MESH = pl.DeviceIdType.MESH
+PARTS = 2
 
 REACH = 2
 FARREACH = 8
@@ -204,19 +205,22 @@
         )
     pl.semaphore_signal(barrier, inc=1, device_id={"grp": other}, device_id_type=MESH)
 
-    def near_copy(buf, stage, source, slot, target, size):
+    def near_copy(buf, stage, source, slot, target, size, part):
+        piece = size // PARTS
         return pltpu.make_async_remote_copy(
-            src_ref=buf.at[pl.ds(source * size, size)],
-            dst_ref=buf.at[pl.ds(slot * size, size)],
-            send_sem=near_send.at[stage, slot],
-            recv_sem=near_recv.at[stage, slot],
+            src_ref=buf.at[pl.ds(source * size + part * piece, piece)],
+            dst_ref=buf.at[pl.ds(slot * size + part * piece, piece)],
+            send_sem=near_send.at[stage, slot, part],
+            recv_sem=near_recv.at[stage, slot, part],
             device_id={"dev": target},
             device_id_type=MESH,
         )
 
     def near_start(buf, stage, size):
-        near_copy(buf, stage, 0, 2, across, size).start()
-        near_copy(buf, stage, 0, 1, mate, size).start()
+        for part in range(PARTS):
+            near_copy(buf, stage, 0, 2, across, size, part).start()
+        for part in range(PARTS):
+            near_copy(buf, stage, 0, 1, mate, size, part).start()
 
         @pl.when(jnp.logical_not(has_z))
         def _():
@@ -227,42 +231,48 @@
             buf[pl.ds(4 * size, size), :] = jnp.zeros((size, buf.shape[1]), buf.dtype)
 
     def near_relay(buf, stage, size):
-        near_copy(buf, stage, 0, 2, across, size).wait_recv()
-
-        @pl.when(sends_z)
-        def _():
-            near_copy(buf, stage, 2, 3, z_target, size).start()
-
-        @pl.when(core == row)
-        def _():
-            near_copy(buf, stage, 2, 4, mate, size).start()
-
-        @pl.when(has_z)
-        def _():
-            near_copy(buf, stage, 2, 3, mate, size).wait_recv()
-
-        @pl.when(has_z & (core != row))
-        def _():
-            near_copy(buf, stage, 3, 4, mate, size).start()
+        for part in range(PARTS):
+            near_copy(buf, stage, 0, 2, across, size, part).wait_recv()
+
+            @pl.when(sends_z)
+            def _():
+                near_copy(buf, stage, 2, 3, z_target, size, part).start()
+
+            @pl.when(core == row)
+            def _():
+                near_copy(buf, stage, 2, 4, mate, size, part).start()
+
+    def near_second(buf, stage, size):
+        for part in range(PARTS):
+
+            @pl.when(has_z)
+            def _():
+                near_copy(buf, stage, 2, 3, mate, size, part).wait_recv()
+
+            @pl.when(has_z & (core != row))
+            def _():
+                near_copy(buf, stage, 3, 4, mate, size, part).start()
 
     def near_finish(buf, stage, size):
-        near_copy(buf, stage, 0, 1, mate, size).wait_recv()
-
-        @pl.when(has_z | (core != row))
-        def _():
-            near_copy(buf, stage, 0, 4, mate, size).wait_recv()
+        for part in range(PARTS):
+            near_copy(buf, stage, 0, 1, mate, size, part).wait_recv()
+
+            @pl.when(has_z | (core != row))
+            def _():
+                near_copy(buf, stage, 0, 4, mate, size, part).wait_recv()
 
     def near_drain(buf, stage, size):
-        near_copy(buf, stage, 0, 1, mate, size).wait_send()
-        near_copy(buf, stage, 0, 2, across, size).wait_send()
-
-        @pl.when(sends_z)
-        def _():
-            near_copy(buf, stage, 2, 3, z_target, size).wait_send()
-
-        @pl.when(has_z | (core == row))
-        def _():
-            near_copy(buf, stage, 0, 4, mate, size).wait_send()
+        for part in range(PARTS):
+            near_copy(buf, stage, 0, 1, mate, size, part).wait_send()
+            near_copy(buf, stage, 0, 2, across, size, part).wait_send()
+
+            @pl.when(sends_z)
+            def _():
+                near_copy(buf, stage, 2, 3, z_target, size, part).wait_send()
+
+            @pl.when(has_z | (core == row))
+            def _():
+                near_copy(buf, stage, 0, 4, mate, size, part).wait_send()
 
     def tree_block(buf, owner, size):
         return buf.at[pl.ds(pl.multiple_of(owner * size, 16), size)]
@@ -312,7 +322,8 @@
             device_id_type=MESH,
         )
 
-    points[pl.ds(0, leaf), :] = coords_ref[...]
+    dim = coords_ref.shape[0]
+    points[pl.ds(0, dim), :] = coords_ref[...]
     transfer_rows = transfer_ref[0]
     packed = rank + 16
     local_cluster = jnp.clip(cluster_ref[0] - group * clusters, 0, clusters - 1)
@@ -328,49 +339,11 @@
             total = total + hit * cluscoup_ref[local_cluster, k].astype(f32)
         mine[:, place * rank : (place + 1) * rank] = total.astype(bf16)
 
-    pl.semaphore_wait(barrier, n)
-    near_start(points, 0, leaf)
-    tree_start(moved, 0, packed)
-    grp_copy(mine, theirs, 0).start()
-
     targets = lax.broadcasted_iota(jnp.int32, (leaf, leaf), 0)
     one_hot = jnp.where(targets == perm_ref[...], 1.0, 0.0).astype(bf16)
     placed = jnp.dot(one_hot, basis_ref[...], preferred_element_type=f32)
     basis_p[...] = placed.astype(bf16)
     basis_t[...] = placed.T.astype(bf16)
-    for place in range(n):
-        total = jnp.zeros((rank, rank), f32)
-        for k in range(far_ref.shape[1]):
-            hit = (far_ref[0, k] == group * n + place).astype(f32)
-            total = total + hit * coup_ref[0, k].astype(f32)
-        chosen[:, place * rank : (place + 1) * rank] = total.astype(bf16)
-
-    last = (((1,), (1,)), ((), ()))
-    left = coords_ref[...]
-    left_sq = jnp.sum(left * left, axis=1, keepdims=True)
-
-    def fill_block(slot, source):
-        right = points[pl.ds(slot * leaf, leaf), :]
-        right_sq = lax.dot_general(
-            jnp.ones((8, right.shape[1]), f32),
-            right * right,
-            last,
-            precision=lax.Precision.HIGHEST,
-            preferred_element_type=f32,
-        )[0:1, :]
-        inner = lax.dot_general(
-            left, right, last, precision=lax.Precision.HIGHEST, preferred_element_type=f32
-        )
-        block = jnp.exp(-kernel_scale * (left_sq + right_sq - 2.0 * inner))
-        if source is not None:
-            wanted = group * n + source
-            hit = jnp.float32(0.0)
-            for k in range(near_ref.shape[1]):
-                listed = (near_ref[0, k] == wanted) & (near_ref[0, k] >= 0)
-                hit = hit + listed.astype(f32)
-            block = hit * block
-        blocks[:, slot * leaf : (slot + 1) * leaf] = block.astype(bf16)
-
     ridge = ridge_ref[...]
     bottom_edge = ridge + spectrum_gap
     top_edge = ridge + spectrum_top
@@ -391,40 +364,79 @@
         tree_start(skel.at[rounds], rounds + 1, rank)
         near_start(wide.at[rounds], rounds + 1, leaf)
 
-    fill_block(0, None)
-    tree_relay(moved, 0, packed)
-    near_relay(points, 0, leaf)
+    pl.semaphore_wait(barrier, n)
+    near_start(points, 0, dim)
     launch(0)
-    near_finish(points, 0, leaf)
-    fill_block(1, mate)
-    fill_block(2, across)
-    tree_finish(moved, 0, packed)
+    tree_start(moved, 0, packed)
+    grp_copy(mine, theirs, 0).start()
+
     for place in range(n):
-        part = moved[place * packed : place * packed + rank, :]
-        for c in range(clusters):
-            tag = moved[place * packed + rank : place * packed + packed, :][c : c + 1, :]
-            spread_t[c * rank : (c + 1) * rank, place * rank : (place + 1) * rank] = (
-                part.astype(f32) * tag.astype(f32)
-            ).astype(bf16)
+        total = jnp.zeros((rank, rank), f32)
+        for k in range(far_ref.shape[1]):
+            hit = (far_ref[0, k] == group * n + place).astype(f32)
+            total = total + hit * coup_ref[0, k].astype(f32)
+        chosen[:, place * rank : (place + 1) * rank] = total.astype(bf16)
+
+    left = coords_ref[...].T
+    left_sq = jnp.sum(left * left, axis=1, keepdims=True)
+
+    def fill_block(slot, source):
+        right = points[pl.ds(slot * dim, dim), :]
+        right_sq = jnp.sum(right * right, axis=0, keepdims=True)
+        inner = jnp.dot(
+            left, right, precision=lax.Precision.HIGHEST, preferred_element_type=f32
+        )
+        block = jnp.exp(-kernel_scale * (left_sq + right_sq - 2.0 * inner))
+        if source is not None:
+            wanted = group * n + source
+            hit = jnp.float32(0.0)
+            for k in range(near_ref.shape[1]):
+                listed = (near_ref[0, k] == wanted) & (near_ref[0, k] >= 0)
+                hit = hit + listed.astype(f32)
+            block = hit * block
+        blocks[:, slot * leaf : (slot + 1) * leaf] = block.astype(bf16)
+
+    def spread_transfers():
+        for place in range(n):
+            part = moved[place * packed : place * packed + rank, :]
+            for c in range(clusters):
+                tag = moved[place * packed + rank : place * packed + packed, :][c : c + 1, :]
+                spread_t[c * rank : (c + 1) * rank, place * rank : (place + 1) * rank] = (
+                    part.astype(f32) * tag.astype(f32)
+                ).astype(bf16)
 
     for rounds in range(ITERS):
         stage = rounds + 1
         if rounds > 0:
             launch(rounds)
+        if rounds == 0:
+            fill_block(0, None)
+            near_relay(points, 0, dim)
+            tree_relay(moved, 0, packed)
+            near_second(points, 0, dim)
         acc[...] = ridge * direction[...] + jnp.dot(
             blocks[:, 0:leaf], wide[rounds, 0:leaf, :], preferred_element_type=f32
         )
         tree_relay(skel.at[rounds], stage, rank)
         near_relay(wide.at[rounds], stage, leaf)
         if rounds == 0:
-            fill_block(3, me - 2 + 4 * row)
-            fill_block(4, me - 1 + 2 * core)
+            near_finish(points, 0, dim)
+            fill_block(1, mate)
+            fill_block(2, across)
+            near_second(wide.at[rounds], stage, leaf)
+            tree_finish(moved, 0, packed)
+            spread_transfers()
             grp_copy(mine, theirs, 0).wait_recv()
+        else:
+            near_second(wide.at[rounds], stage, leaf)
         tree_finish(skel.at[rounds], stage, rank)
         sums = jnp.dot(spread_t[...], skel[rounds], preferred_element_type=f32).astype(bf16)
         coup_out[rounds] = jnp.dot(theirs[...], sums, preferred_element_type=f32).astype(bf16)
         grp_copy(coup_out.at[rounds], coup_in.at[rounds], stage).start()
         level_one = jnp.dot(chosen[...], skel[rounds], preferred_element_type=f32)
+        if rounds == 0:
+            fill_block(3, me - 2 + 4 * row)
+            fill_block(4, me - 1 + 2 * core)
         near_finish(wide.at[rounds], stage, leaf)
         acc[...] += jnp.dot(
             blocks[:, leaf:], wide[rounds, leaf:, :], preferred_element_type=f32
@@ -442,7 +454,7 @@
         sol_ref[...] += moved_on
         contraction = rho_next
 
-    near_drain(points, 0, leaf)
+    near_drain(points, 0, dim)
     tree_drain(moved, 0, packed)
     grp_copy(mine, theirs, 0).wait_send()
     for rounds in range(ITERS):
@@ -482,7 +494,7 @@
         in_specs=[vmem, vmem, vmem, smem, smem, vmem, vmem, vmem, smem, smem, vmem, vmem],
         out_specs=(vmem, vmem),
         scratch_shapes=[
-            pltpu.VMEM((5 * leaf, dim), f32),
+            pltpu.VMEM((5 * dim, leaf), f32),
             pltpu.VMEM((ITERS, 5 * leaf, outs), bf16),
             pltpu.VMEM((leaf, 5 * leaf), bf16),
             pltpu.VMEM((ITERS, n * rank, outs), bf16),
@@ -497,8 +509,8 @@
             pltpu.VMEM((rank, leaf), bf16),
             pltpu.VMEM((leaf, outs), f32),
             pltpu.VMEM((leaf, outs), f32),
-            sem((stages, 5)),
-            sem((stages, 5)),
+            sem((stages, 5, PARTS)),
+            sem((stages, 5, PARTS)),
             sem((stages, n // 2)),
             sem((stages, n // 2)),
             sem((stages, n // 2)),
@@ -511,7 +523,7 @@
         ),
         name="fused_solve",
     )(
-        coords,
+        coords.T,
         right_side,
         leaf_perm,
         near_list,

time: 81 us -> 76 us (0.938)
  Pallas kernels: 73.7 us -> 65.8 us
  local copies, waits for them, and re-layouts: 4.86 us -> 7.78 us
    pallas_call x1, Pallas kernels: 73.7 us -> 65.8 us  [fused_body(): pl.pallas_call(functools.partial(fused_kernel, n), out_shape=(out, out),...]
    unnamed x21 -> x22, local copies, waits for them, and re-layouts: 4.86 us -> 7.78 us
where the time goes in v2:
time: 76 us; the launch traced here: 75.6 us
  Pallas kernels  65.8 us (87%)
  local copies, waits for them, and re-layouts  7.78 us (10%)
  between operations  2.01 us (3%)
    pallas_call x1, Pallas kernels, fused_body(): pl.pallas_call(functools.partial(fused_kernel, n), out_shape=(out, out),...  65.8 us
    unnamed x22, local copies, waits for them, and re-layouts  7.78 us

profile of v2, /device:TPU:4, one launch (start us, length us, event | category | flops | bytes accessed | tf_op | source)
XLA Modules:
  0.0 75.6 jit_solution(16132241344496497492)
XLA Ops:
  1.3 0.0 copy-start.7
  1.3 0.0 copy-start.6
  2.0 0.0 copy-start.8
  2.0 0.0 copy-start.9
  2.0 0.0 copy-done.7
  2.0 0.0 copy-done.6
  2.0 0.6 copy-done.8
  2.6 0.0 copy-done.9
  2.6 0.0 copy-start
  2.6 1.0 %copy-done = f32[512,256]{1,0:T(8,128)S(1)} copy-done((f32[512,256]{1,0:T(8,128)S(1)}, f32[512,256]{1,0:T(8,128)}, u32[]{:S(2)}) %copy-start) | copy-done | bytes 524312
  3.7 0.0 copy-start.1
  3.7 1.0 %copy-done.1 = bf16[4,4,128,128]{3,2,1,0:T(8,128)(2,1)S(1)} copy-done((bf16[4,4,128,128]{3,2,1,0:T(8,128)(2,1)S(1)}, bf16[4,4,128,128]{3,2,1,0:T(8,128)(2,1)}, u32[]{:S(2)}) %copy-start.1) | copy-done | bytes 524312
  4.7 0.0 copy-start.2
  4.7 0.9 %copy-done.2 = f32[512,64]{0,1:T(8,128)S(1)} copy-done((f32[512,64]{0,1:T(8,128)S(1)}, f32[512,64]{0,1:T(8,128)}, u32[]{:S(2)}) %copy-start.2) | copy-done | bytes 131096
  5.6 0.0 copy-start.3
  5.6 0.9 %copy-done.3 = bf16[1,4,128,128]{3,2,1,0:T(8,128)(2,1)S(1)} copy-done((bf16[1,4,128,128]{3,2,1,0:T(8,128)(2,1)S(1)}, bf16[1,4,128,128]{3,2,1,0:T(8,128)(2,1)}, u32[]{:S(2)}) %copy-start.3) | copy-done | bytes 131096
  6.5 0.0 copy-start.4
  6.5 0.9 %copy-done.4 = bf16[512,128]{1,0:T(8,128)(2,1)S(1)} copy-done((bf16[512,128]{1,0:T(8,128)(2,1)S(1)}, bf16[512,128]{1,0:T(8,128)(2,1)}, u32[]{:S(2)}) %copy-start.4) | copy-done | bytes 131096
  7.4 0.0 copy-start.5
  7.4 0.8 copy-done.5
  8.2 65.8 %fused_solve.1 = (f32[512,256]{1,0:T(8,128)S(1)}, f32[512,256]{1,0:T(8,128)S(1)}) custom-call(f32[64,512]{1,0:T(8,128)S(1)} %bitcast.3, f32[512,256]{1,0:T(8,128)S(1)} %copy-done, s32[1,512]{1,0:T(1,128)S(1)} %copy-done.6, s32[1,4]{1,0:T(1,128)S(1)} %copy-done.8, s32[1,4]{1,0:T(1,128)S(1)} %copy-done.9, bf16[1,4,128,128]{3,2,1,0:T(8,128)(2,1)S(1)} %copy-done.3, ...), custom_call_target="tpu_custom_call" | custom-call | tf_op jit(solution)/shard_map/fused_solve/pallas_call | solution.py:491
  74.0 0.8 %copy.18 = f32[512,256]{1,0:T(8,128)} copy(f32[512,256]{1,0:T(8,128)S(1)} %get-tuple-element.4) | data formatting | bytes 1048576
  74.8 0.8 %copy.19 = f32[512,256]{1,0:T(8,128)} copy(f32[512,256]{1,0:T(8,128)S(1)} %get-tuple-element.5) | data formatting | bytes 1048576
Async XLA Ops:
  1.3 0.7 copy-start.7
  1.3 0.7 copy-start.6
  2.0 0.7 copy-start.8
  2.0 0.7 copy-start.9
  2.6 1.0 %copy-start = (f32[512,256]{1,0:T(8,128)S(1)}, f32[512,256]{1,0:T(8,128)}, u32[]{:S(2)}) copy-start(f32[512,256]{1,0:T(8,128)} %right_ref.1) | copy-start | bytes 1572868
  3.7 1.0 %copy-start.1 = (bf16[4,4,128,128]{3,2,1,0:T(8,128)(2,1)S(1)}, bf16[4,4,128,128]{3,2,1,0:T(8,128)(2,1)}, u32[]{:S(2)}) copy-start(bf16[4,4,128,128]{3,2,1,0:T(8,128)(2,1)} %cluscoup_ref.1) | copy-start | bytes 1572868
  4.7 0.9 %copy-start.2 = (f32[512,64]{0,1:T(8,128)S(1)}, f32[512,64]{0,1:T(8,128)}, u32[]{:S(2)}) copy-start(f32[512,64]{0,1:T(8,128)} %param.12) | copy-start | bytes 393220
  5.6 0.9 %copy-start.3 = (bf16[1,4,128,128]{3,2,1,0:T(8,128)(2,1)S(1)}, bf16[1,4,128,128]{3,2,1,0:T(8,128)(2,1)}, u32[]{:S(2)}) copy-start(bf16[1,4,128,128]{3,2,1,0:T(8,128)(2,1)} %coup_ref.1) | copy-start | bytes 393220
  6.5 0.9 %copy-start.4 = (bf16[512,128]{1,0:T(8,128)(2,1)S(1)}, bf16[512,128]{1,0:T(8,128)(2,1)}, u32[]{:S(2)}) copy-start(bf16[512,128]{1,0:T(8,128)(2,1)} %basis_ref.1) | copy-start | bytes 393220
  7.4 0.8 %copy-start.5 = (bf16[1,128,128]{2,1,0:T(8,128)(2,1)S(1)}, bf16[1,128,128]{2,1,0:T(8,128)(2,1)}, u32[]{:S(2)}) copy-start(bf16[1,128,128]{2,1,0:T(8,128)(2,1)} %transfer_ref.1) | copy-start | bytes 98308

commit v3 on v2

--- a/solution.py
+++ b/solution.py
@@ -287,23 +287,40 @@
             device_id_type=MESH,
         )
 
-    def same_core(step):
-        return lax.rem(chip + step + chips, chips) * 2 + core
+    planes = chips // 2
+    plane = lax.div(chip, 2)
+
+    def along(step):
+        return (lax.rem(plane + step % planes, planes) * 2 + row) * 2 + core
+
+    def owner_of(step, side):
+        flipped = row if step < planes else 1 - row
+        return (lax.rem(plane - step % planes + planes, planes) * 2 + flipped) * 2 + side
 
     def tree_start(buf, stage, size):
-        for step in range(1, chips):
-            tree_copy(buf, stage, step, me, same_core(step), size, tree_send, tree_recv).start()
+        tree_copy(buf, stage, planes, me, across, size, tree_send, tree_recv).start()
+        for step in range(1, planes):
+            tree_copy(buf, stage, step, me, along(step), size, tree_send, tree_recv).start()
         tree_copy(buf, stage, 0, me, mate, size, mate_send, mate_recv).start()
 
+    def tree_pass(buf, stage, step, size):
+        owner = owner_of(step, core)
+        tree_copy(buf, stage, step, owner, mate, size, mate_send, mate_recv).start()
+
     def tree_relay(buf, stage, size):
-        for step in range(1, chips):
-            owner = same_core(-step)
+        for step in (planes, *range(1, planes), *range(planes + 1, chips)):
+            owner = owner_of(step, core)
             tree_copy(buf, stage, step, owner, mate, size, tree_send, tree_recv).wait_recv()
-            tree_copy(buf, stage, step, owner, mate, size, mate_send, mate_recv).start()
+            if step == planes:
+                for later in range(planes + 1, chips):
+                    tree_copy(
+                        buf, stage, later, across, along(later), size, tree_send, tree_recv
+                    ).start()
+            tree_pass(buf, stage, step, size)
 
     def tree_finish(buf, stage, size):
         for step in range(chips):
-            owner = lax.rem(chip - step + chips, chips) * 2 + (1 - core)
+            owner = owner_of(step, 1 - core)
             tree_copy(buf, stage, step, owner, mate, size, mate_send, mate_recv).wait_recv()
 
     def tree_drain(buf, stage, size):

time: 76 us -> 74.8 us (0.984)
  Pallas kernels: 65.8 us -> 64.6 us
    pallas_call x1, Pallas kernels: 65.8 us -> 64.6 us  [fused_body(): pl.pallas_call(functools.partial(fused_kernel, n), out_shape=(out, out),...]
where the time goes in v3:
time: 74.8 us; the launch traced here: 74.4 us
  Pallas kernels  64.6 us (86%)
  local copies, waits for them, and re-layouts  7.78 us (10%)
  between operations  2.01 us (3%)
    pallas_call x1, Pallas kernels, fused_body(): pl.pallas_call(functools.partial(fused_kernel, n), out_shape=(out, out),...  64.6 us
    unnamed x22, local copies, waits for them, and re-layouts  7.78 us

profile of v3, /device:TPU:4, one launch (start us, length us, event | category | flops | bytes accessed | tf_op | source)
XLA Modules:
  0.0 74.4 jit_solution(57877308439913354)
XLA Ops:
  1.3 0.0 copy-start.7
  1.3 0.0 copy-start.6
  2.0 0.0 copy-start.8
  2.0 0.0 copy-start.9
  2.0 0.0 copy-done.7
  2.0 0.0 copy-done.6
  2.0 0.6 copy-done.8
  2.6 0.0 copy-done.9
  2.6 0.0 copy-start
  2.6 1.0 %copy-done = f32[512,256]{1,0:T(8,128)S(1)} copy-done((f32[512,256]{1,0:T(8,128)S(1)}, f32[512,256]{1,0:T(8,128)}, u32[]{:S(2)}) %copy-start) | copy-done | bytes 524312
  3.7 0.0 copy-start.1
  3.7 1.0 %copy-done.1 = bf16[4,4,128,128]{3,2,1,0:T(8,128)(2,1)S(1)} copy-done((bf16[4,4,128,128]{3,2,1,0:T(8,128)(2,1)S(1)}, bf16[4,4,128,128]{3,2,1,0:T(8,128)(2,1)}, u32[]{:S(2)}) %copy-start.1) | copy-done | bytes 524312
  4.7 0.0 copy-start.2
  4.7 0.9 %copy-done.2 = f32[512,64]{0,1:T(8,128)S(1)} copy-done((f32[512,64]{0,1:T(8,128)S(1)}, f32[512,64]{0,1:T(8,128)}, u32[]{:S(2)}) %copy-start.2) | copy-done | bytes 131096
  5.6 0.0 copy-start.3
  5.6 0.9 %copy-done.3 = bf16[1,4,128,128]{3,2,1,0:T(8,128)(2,1)S(1)} copy-done((bf16[1,4,128,128]{3,2,1,0:T(8,128)(2,1)S(1)}, bf16[1,4,128,128]{3,2,1,0:T(8,128)(2,1)}, u32[]{:S(2)}) %copy-start.3) | copy-done | bytes 131096
  6.5 0.0 copy-start.4
  6.5 0.9 %copy-done.4 = bf16[512,128]{1,0:T(8,128)(2,1)S(1)} copy-done((bf16[512,128]{1,0:T(8,128)(2,1)S(1)}, bf16[512,128]{1,0:T(8,128)(2,1)}, u32[]{:S(2)}) %copy-start.4) | copy-done | bytes 131096
  7.4 0.0 copy-start.5
  7.4 0.8 %copy-done.5 = bf16[1,128,128]{2,1,0:T(8,128)(2,1)S(1)} copy-done((bf16[1,128,128]{2,1,0:T(8,128)(2,1)S(1)}, bf16[1,128,128]{2,1,0:T(8,128)(2,1)}, u32[]{:S(2)}) %copy-start.5) | copy-done | bytes 32792
  8.2 64.6 %fused_solve.1 = (f32[512,256]{1,0:T(8,128)S(1)}, f32[512,256]{1,0:T(8,128)S(1)}) custom-call(f32[64,512]{1,0:T(8,128)S(1)} %bitcast.3, f32[512,256]{1,0:T(8,128)S(1)} %copy-done, s32[1,512]{1,0:T(1,128)S(1)} %copy-done.6, s32[1,4]{1,0:T(1,128)S(1)} %copy-done.8, s32[1,4]{1,0:T(1,128)S(1)} %copy-done.9, bf16[1,4,128,128]{3,2,1,0:T(8,128)(2,1)S(1)} %copy-done.3, ...), custom_call_target="tpu_custom_call" | custom-call | tf_op jit(solution)/shard_map/fused_solve/pallas_call | solution.py:508
  72.8 0.8 %copy.18 = f32[512,256]{1,0:T(8,128)} copy(f32[512,256]{1,0:T(8,128)S(1)} %get-tuple-element.4) | data formatting | bytes 1048576
  73.6 0.8 %copy.19 = f32[512,256]{1,0:T(8,128)} copy(f32[512,256]{1,0:T(8,128)S(1)} %get-tuple-element.5) | data formatting | bytes 1048576
Async XLA Ops:
  1.3 0.7 copy-start.7
  1.3 0.7 copy-start.6
  2.0 0.7 copy-start.8
  2.0 0.7 copy-start.9
  2.6 1.0 %copy-start = (f32[512,256]{1,0:T(8,128)S(1)}, f32[512,256]{1,0:T(8,128)}, u32[]{:S(2)}) copy-start(f32[512,256]{1,0:T(8,128)} %right_ref.1) | copy-start | bytes 1572868
  3.7 1.0 %copy-start.1 = (bf16[4,4,128,128]{3,2,1,0:T(8,128)(2,1)S(1)}, bf16[4,4,128,128]{3,2,1,0:T(8,128)(2,1)}, u32[]{:S(2)}) copy-start(bf16[4,4,128,128]{3,2,1,0:T(8,128)(2,1)} %cluscoup_ref.1) | copy-start | bytes 1572868
  4.7 0.9 %copy-start.2 = (f32[512,64]{0,1:T(8,128)S(1)}, f32[512,64]{0,1:T(8,128)}, u32[]{:S(2)}) copy-start(f32[512,64]{0,1:T(8,128)} %param.12) | copy-start | bytes 393220
  5.6 0.9 %copy-start.3 = (bf16[1,4,128,128]{3,2,1,0:T(8,128)(2,1)S(1)}, bf16[1,4,128,128]{3,2,1,0:T(8,128)(2,1)}, u32[]{:S(2)}) copy-start(bf16[1,4,128,128]{3,2,1,0:T(8,128)(2,1)} %coup_ref.1) | copy-start | bytes 393220
  6.5 0.9 %copy-start.4 = (bf16[512,128]{1,0:T(8,128)(2,1)S(1)}, bf16[512,128]{1,0:T(8,128)(2,1)}, u32[]{:S(2)}) copy-start(bf16[512,128]{1,0:T(8,128)(2,1)} %basis_ref.1) | copy-start | bytes 393220
  7.4 0.8 %copy-start.5 = (bf16[1,128,128]{2,1,0:T(8,128)(2,1)S(1)}, bf16[1,128,128]{2,1,0:T(8,128)(2,1)}, u32[]{:S(2)}) copy-start(bf16[1,128,128]{2,1,0:T(8,128)(2,1)} %transfer_ref.1) | copy-start | bytes 98308
